TPU v7x, 32 devices: a whole 2x2x4 slice. The times are simulated.
32 devices in a mesh: wide: 8 (over z, x), narrow: 4 (over y, core).
Axes of the slice: x: 2, y: 2, z: 4, core: 2. Of those that a mesh axis runs over, the one named last changes fastest.
Arguments:
- a_blocks: float32 [6144, 128, 128], P(('wide', 'narrow')), may hold values from -0.8 to 0.8
- row_map: int32 [6144, 128], P(('wide', 'narrow')), may hold values from 0 to 127
- col_map: int32 [6144, 128], P(('wide', 'narrow')), may hold values from 0 to 127
- target: int32 [6144], P(('wide', 'narrow')), may hold values from 0 to 839
- counts: int32 [8], P('wide'), may hold values from 1 to 8, as said below
- weights: int32 [64], P('wide'), may hold values from 1 to 999
Outputs:
- coarse: float32 [64, 128, 128], P('wide', 'narrow')
- work_offset: int32 [64], P('wide')
Inputs may be any that keep to these rules, and one draw needn't show every extreme that they name: `counts`: every index of wide has at least one live slot and at most 8; some index has exactly 8; the last index has fewer than 8.
All inputs are finite; a program needn't handle non-finite values.
Results may differ from a plain program's by a relative error of at most 0.0003.
Values sent between devices are 32-bit elements; how exact they have to be, the bound alone decides.
No kernel may reach another device: no remote copies, remote signals or barrier semaphores. Data moves between devices by JAX's collectives and lax.ppermute only.
A program may use at most 128 MiB of HBM per device.

v0:
```python
import jax
import jax.numpy as jnp
from jax import lax
from jax.sharding import PartitionSpec as P


def local(a_blocks, row_map, col_map, target, counts, weights):
    block_size = a_blocks.shape[1]
    slot_count = weights.shape[0]
    nwide = lax.axis_size("wide")
    own_index = lax.axis_index("wide")
    live_count = counts[0]
    slot_of = target % live_count
    target_positions = jnp.arange(slot_count, dtype=jnp.int32)
    is_live = target_positions < live_count
    live_weight = jnp.where(is_live, weights, 0)
    local_total = jnp.sum(live_weight)
    table = lax.all_gather(
        jnp.stack([live_count, local_total])[None, :], "wide", axis=0, tiled=True
    )
    upper = jnp.arange(nwide, dtype=jnp.int32) > own_index
    higher_count = jnp.sum(jnp.where(upper, table[:, 0], 0))
    higher_weight = jnp.sum(jnp.where(upper, table[:, 1], 0))
    start = nwide * slot_count - higher_count - live_count
    inner = jnp.arange(block_size, dtype=jnp.int32)
    row_onehot = (row_map[:, :, None] == inner[None, None, :]).astype(jnp.float32)
    col_onehot = (col_map[:, :, None] == inner[None, None, :]).astype(jnp.float32)
    merged = jnp.einsum("brc,bcd->brd", a_blocks, col_onehot, precision=lax.Precision.HIGHEST)
    reduced = jnp.einsum("bre,brd->bed", row_onehot, merged, precision=lax.Precision.HIGHEST)
    select = (slot_of[:, None] == target_positions[None, :]).astype(jnp.float32)
    partial_value = jnp.einsum("bs,bed->sed", select, reduced, precision=lax.Precision.HIGHEST)
    accumulated_sum = lax.psum_scatter(partial_value, "narrow", scatter_dimension=1, tiled=True)
    destination = jnp.where(is_live, start + target_positions, -1)
    offset_of = jnp.where(is_live, higher_weight + local_total - jnp.cumsum(live_weight), 0)
    blocks_in = lax.all_gather(accumulated_sum, "wide", axis=0, tiled=True)
    entry_index = lax.all_gather(destination, "wide", axis=0, tiled=True)
    offset_in = lax.all_gather(offset_of, "wide", axis=0, tiled=True)
    local_position = entry_index - own_index * slot_count
    pick = local_position[None, :] == target_positions[:, None]
    blocks_acc = jnp.einsum(
        "sk,kjm->sjm", pick.astype(jnp.float32), blocks_in, precision=lax.Precision.HIGHEST
    )
    offset_acc = jnp.sum(jnp.where(pick, offset_in[None, :], 0), axis=1).astype(jnp.int32)
    return (blocks_acc, offset_acc)


def solution(mesh):
    return jax.shard_map(
        local,
        mesh=mesh,
        in_specs=(
            P(("wide", "narrow"), None, None),
            P(("wide", "narrow"), None),
            P(("wide", "narrow"), None),
            P(("wide", "narrow")),
            P("wide"),
            P("wide"),
        ),
        out_specs=(P("wide", "narrow", None), P("wide")),
        check_vma=False,
    )
```

profile of v0, /device:TPU:0, one launch (start us, length us, event | category | flops | bytes accessed | tf_op | source)
XLA Modules:
  0.0 140.8 jit_solution(8387390500596582619)
XLA Ops:
  7.2 0.0 reduce-scatter.2.cloned.1.call-start
  7.9 0.0 copy-start
  7.9 21.2 %fusion.4 = f32[192,128,128]{2,1,0:T(8,128)S(1)} fusion(f32[192,128,128]{2,1,0:T(8,128)} %param.6, s32[192,128]{1,0:T(8,128)} %param.8), kind=kOutput, calls=%fused_computation.6 | convolution fusion | flops 4838129664 | bytes 25264128 | tf_op jit(solution)/shard_map/brc,bcd->brd/dot_general | solution.py:28
  29.0 0.0 copy-done
  29.0 0.0 copy-start.1
  29.1 20.3 %fusion.6 = f32[192,128,128]{2,1,0:T(8,128)} fusion(f32[192,128,128]{2,1,0:T(8,128)S(1)} %fusion.4, s32[192,128]{1,0:T(8,128)S(1)} %copy-done), kind=kOutput, calls=%fused_computation.7 | convolution fusion | flops 4838129664 | bytes 25264128 | tf_op jit(solution)/shard_map/bre,brd->bed/dot_general | solution.py:29
  49.3 0.0 copy-start.3
  49.3 0.0 copy-start.2
  49.3 0.0 copy-done.1
  49.3 0.1 and_select_fusion
  49.4 16.1 %fusion = f32[8,128,128]{2,0,1:T(8,128)} fusion(f32[192,128,128]{2,1,0:T(8,128)} %fusion.6, s32[192]{0:T(256)S(1)} %and_select_fusion), kind=kOutput, calls=%fused_computation | convolution fusion | flops 301991424 | bytes 13107968 | tf_op jit(solution)/shard_map/bs,bed->sed/dot_general | solution.py:31
  65.6 0.0 reduce-scatter.2.cloned.1.call-update
  65.6 0.0 all-gather.3.cloned.1.call-start
  65.7 24.5 %reduce-scatter.2.cloned.1.call-done = f32[8,32,128]{2,0,1:T(8,128)} async-done(((f32[8,128,128]{2,0,1:T(8,128)}), f32[8,32,128]{2,0,1:T(8,128)}) %reduce-scatter.2.cloned.1.call-update) | async-done | bytes 131088 | tf_op jit(solution)/shard_map/reduce_scatter | solution.py:32
  90.1 0.0 all-gather.3.cloned.1.call-update
  90.2 0.0 copy-done.3
  90.2 0.6 dynamic-slice
  91.4 0.0 copy-done.2
  91.4 0.7 fusion.21
  92.1 0.8 add_dynamic-update-slice_fusion
  92.9 11.4 %all-reduce = s32[16]{0:T(128)S(1)} all-reduce(s32[16]{0:T(128)S(1)} %add_dynamic-update-slice_fusion), channel_id=2, replica_groups=mesh['wide'=8,'narrow'=4] {'wide'}, use_global_device_ids=true, to_apply=%add | all-reduce | flops 16 | bytes 128
  105.0 0.1 reshape.36
  105.0 0.2 slice_reduce_fusion
  105.2 0.7 fusion.17
  107.7 0.2 reduce-window.9
  107.9 0.1 select_dynamic-update-slice_fusion
  108.0 0.1 fusion.19
  108.1 8.4 %all-reduce.3 = (s32[64]{0:T(128)S(1)}, s32[64]{0:T(128)S(1)}) all-reduce(s32[64]{0:T(128)S(1)} %select_dynamic-update-slice_fusion, s32[64]{0:T(128)S(1)} %fusion.19), channel_id=1, replica_groups=mesh['wide'=8,'narrow'=4] {'wide'}, use_global_device_ids=true, to_apply=%add.1 | all-reduce | flops 128 | bytes 1024
  116.6 0.6 select_reduce_fusion
  117.2 14.4 %all-gather.3.cloned.1.call-done = f32[64,32,128]{2,0,1:T(8,128)} async-done(((f32[8,32,128]{2,0,1:T(8,128)}), f32[64,32,128]{2,0,1:T(8,128)}) %all-gather.3.cloned.1.call-update) | async-done | bytes 1048592 | tf_op jit(solution)/shard_map/all_gather | solution.py:35
  131.6 1.7 %fusion.14 = f32[8,32,128]{2,0,1:T(8,128)S(1)} fusion(f32[64,32,128]{2,0,1:T(8,128)} %all-gather.3.cloned.1.call-done, s32[64]{0:T(128)S(1)} %broadcast_subtract_fusion), kind=kOutput, calls=%fused_computation.18 | convolution fusion | flops 25166336 | bytes 1179904 | tf_op jit(solution)/shard_map/sk,kjm->sjm/dot_general | solution.py:40
  133.3 0.7 copy.9
  (4 shorter events, 0.0 us)
Async XLA Ops:
  7.2 83.0 %reduce-scatter.2.cloned.1.call-start = ((), (), s32[]{:S(2)}) async-start(), calls=%async_computation.1 | async-start | bytes 655360 | tf_op jit(solution)/shard_map/reduce_scatter | solution.py:32
  7.9 21.2 %copy-start = (s32[192,128]{1,0:T(8,128)S(1)}, s32[192,128]{1,0:T(8,128)}, u32[]{:S(2)}) copy-start(s32[192,128]{1,0:T(8,128)} %param.7) | copy-start | bytes 294916
  29.0 20.3 %copy-start.1 = (s32[192]{0:T(256)S(1)}, s32[192]{0:T(256)}, u32[]{:S(2)}) copy-start(s32[192]{0:T(256)} %param.9) | copy-start | bytes 2308
  49.3 40.9 %copy-start.3 = (u32[32]{0:T(128)S(1)}, u32[32]{0:T(128)}, u32[]{:S(2)}) copy-start(u32[32]{0:T(128)} %constant.27) | copy-start | bytes 388
  49.3 42.1 %copy-start.2 = (s32[8]{0:T(128)S(1)}, s32[8]{0:T(128)}, u32[]{:S(2)}) copy-start(s32[8]{0:T(128)} %param.11) | copy-start | bytes 100
  65.6 66.0 %all-gather.3.cloned.1.call-start = ((), (), s32[]{:S(2)}) async-start(), calls=%async_computation.2 | async-start | bytes 1179648 | tf_op jit(solution)/shard_map/all_gather | solution.py:35
Sparse Core Ops, SparseCore 0:
  65.7 24.3 reduce-scatter.1
  92.2 39.3 all-gather.2
where the time goes:
time: 141 us
  matrix products  59.2 us (42%)
  waiting for transfers between devices  38.9 us (28%)
  blocking collectives  19.8 us (14%)
  between operations  17.9 us (13%)
  other arithmetic  3.27 us (2%)
  local copies, waits for them, and re-layouts  1.55 us (1%)
    reduce_scatter x1, waiting for transfers between devices, local(): lax.psum_scatter(partial_value, 'narrow', scatter_dimension=1, tiled=True)  24.5 us
    dot_general x1, matrix products, local(): jnp.einsum('brc,bcd->brd', a_blocks, col_onehot, precision=lax.Precision....  21.2 us
    dot_general x1, matrix products, local(): jnp.einsum('bre,brd->bed', row_onehot, merged, precision=lax.Precision.HI...  20.3 us
    unnamed x2, blocking collectives  19.8 us
    dot_general x1, matrix products, local(): jnp.einsum('bs,bed->sed', select, reduced, precision=lax.Precision.HIGHEST)  16.1 us
    all_gather x1, waiting for transfers between devices, local(): blocks_in = lax.all_gather(accumulated_sum, 'wide', axis=0, tiled=True)  14.4 us
  transfers between devices with their start and end apart: 2, of which 2 were waited for; matrix products, arithmetic and copies ran while one was open for 3% of the time, Pallas kernels for 0%

commit v1 on v0

v1 whole, which is shorter than its diff:
```python
import functools

import jax
import jax.numpy as jnp
from jax import lax
from jax.experimental import pallas as pl
from jax.experimental.pallas import tpu as pltpu
from jax.sharding import PartitionSpec as P

F32, BF16 = jnp.float32, jnp.bfloat16
NT = (((1,), (1,)), ((), ()))


def split(a):
    hi = a.astype(BF16)
    return hi, (a - hi.astype(F32)).astype(BF16)


def onehot(vec, pos):
    return jnp.where(vec.astype(F32).astype(BF16) == pos, jnp.ones((), BF16), jnp.zeros((), BF16))


def coarsen_body(slot_ref, me_ref, a_ref, row_ref, col_ref, *outs, places, rows):
    i = pl.program_id(0)
    group, n, _ = a_ref.shape

    @pl.when(i == 0)
    def _():
        for o in outs:
            o[...] = jnp.zeros_like(o)

    iota = lax.broadcasted_iota(jnp.int32, (n, n), 0)
    row_pos = ((iota // rows) ^ me_ref[0]) * rows + iota % rows
    row_pos = row_pos.astype(F32).astype(BF16)
    col_pos = iota.astype(F32).astype(BF16)
    for g in range(group):
        r = onehot(row_ref[g : g + 1, :], row_pos)
        c = onehot(col_ref[g : g + 1, :], col_pos)
        y = jnp.dot(
            jnp.concatenate([r, r], 1), jnp.concatenate(split(a_ref[g]), 0), preferred_element_type=F32
        )
        x = lax.dot_general(
            jnp.concatenate(split(y), 1), jnp.concatenate([c, c], 1), NT, preferred_element_type=F32
        )
        s = slot_ref[i * group + g]
        for rel, (k, b) in enumerate(places):
            outs[k][b, s] += x[rel * rows : (rel + 1) * rows]


def coarsen(slot_of, me, a_blocks, row_map, col_map, slots, parts):
    count, n, _ = a_blocks.shape
    rows = n // parts
    stages = parts.bit_length() - 1
    group = max(g for g in range(8, 49, 8) if count % g == 0)
    places, sizes = [], [0] * (stages + 1)
    for rel in range(parts):
        k = stages if rel == 0 else (rel & -rel).bit_length() - 1
        places.append((k, sizes[k]))
        sizes[k] += 1
    return pl.pallas_call(
        functools.partial(coarsen_body, places=places, rows=rows),
        out_shape=[jax.ShapeDtypeStruct((m, slots, rows, n), F32) for m in sizes],
        grid_spec=pltpu.PrefetchScalarGridSpec(
            num_scalar_prefetch=2,
            grid=(count // group,),
            in_specs=[
                pl.BlockSpec((group, n, n), lambda i, s, m: (i, 0, 0)),
                pl.BlockSpec((group, n), lambda i, s, m: (i, 0)),
                pl.BlockSpec((group, n), lambda i, s, m: (i, 0)),
            ],
            out_specs=[pl.BlockSpec((m, slots, rows, n), lambda i, s, m_: (0, 0, 0, 0)) for m in sizes],
        ),
        compiler_params=pltpu.CompilerParams(dimension_semantics=("arbitrary",)),
        cost_estimate=pl.CostEstimate(
            flops=count * 8 * n**3, bytes_accessed=count * n * n * 4, transcendentals=0
        ),
        name="coarsen",
    )(slot_of, me[None], a_blocks, row_map, col_map)


def exchange(x, axis, bit):
    size = lax.axis_size(axis)
    return lax.ppermute(x, axis, [(i, i ^ bit) for i in range(size)])


def local(a_blocks, row_map, col_map, target, counts, weights):
    slots = weights.shape[0]
    parts = lax.axis_size("narrow")
    nwide = lax.axis_size("wide")
    own = lax.axis_index("wide")
    me = lax.axis_index("narrow")
    bits = [1 << k for k in range(nwide.bit_length() - 1)]

    table = jnp.concatenate([counts, weights])[None, :]
    for bit in bits:
        table = jnp.concatenate([table, exchange(table, "wide", bit)], 0)

    slot_of = target % counts[0]
    outs = coarsen(slot_of, me, a_blocks, row_map, col_map, slots, parts)

    owner = own ^ jnp.arange(nwide, dtype=jnp.int32)
    count_of = table[:, 0]
    later = owner[None, :] >= owner[:, None]
    suffix = jnp.sum(jnp.where(later, count_of[None, :], 0), 1)
    start = nwide * slots - suffix
    shift = start[0] % slots
    slot = jnp.arange(slots, dtype=jnp.int32)
    live = slot[None, :] < count_of[:, None]
    place = jnp.where(live, start[:, None] + slot[None, :], -slots).reshape(-1)
    source = jnp.broadcast_to(owner[:, None], (nwide, slots)).reshape(-1)
    weight_of = table[:, 1:].reshape(-1)
    lane, dest = place % slots, place // slots
    at = slot[:, None] == lane[None, :]
    valid = jnp.any(at & (dest == own)[None, :], 1)
    above = place[None, :] > (own * slots + slot)[:, None]
    offset = jnp.where(valid, jnp.sum(jnp.where(above, weight_of[None, :], 0), 1), 0)
    takes, before = [], source
    for bit in bits:
        low = 2 * bit - 1
        after = (source & ~low) | (dest & low)
        moves = (place >= 0) & (after == own) & (before != own)
        takes.append(jnp.any(at & moves[None, :], 1))
        before = after

    outs = [list(o) for o in outs]
    stages = len(outs) - 1
    own_sum = outs[stages][0]
    rels = [[r for r in range(parts) if r and (r & -r) == 1 << k] for k in range(stages)]
    piece = {0: own_sum}
    for k in range(stages):
        for b, rel in enumerate(rels[k]):
            piece[rel] = outs[k][b]
    for k in range(stages):
        for rel in reversed(rels[k]):
            piece[rel ^ (1 << k)] = piece[rel ^ (1 << k)] + exchange(piece[rel], "narrow", 1 << k)
    value = piece[0]

    value = jnp.roll(value, shift, axis=0)
    for bit, take in zip(bits, takes):
        value = jnp.where(take[:, None, None], exchange(value, "wide", bit), value)
    value = jnp.where(valid[:, None, None], value, 0.0)
    return value, offset.astype(jnp.int32)


def solution(mesh):
    return jax.shard_map(
        local,
        mesh=mesh,
        in_specs=(
            P(("wide", "narrow"), None, None),
            P(("wide", "narrow"), None),
            P(("wide", "narrow"), None),
            P(("wide", "narrow")),
            P("wide"),
            P("wide"),
        ),
        out_specs=(P("wide", "narrow", None), P("wide")),
        check_vma=False,
    )
```

time: 141 us -> 53.1 us (0.38)
  matrix products: 59.2 us -> 0 us
  waiting for transfers between devices: 38.9 us -> 18.7 us
  blocking collectives: 19.8 us -> 0 us
  between operations: 17.9 us -> 1.52 us
  starting transfers between devices: 0.08 us -> 13.6 us
  Pallas kernels: 0 us -> 11.1 us
  other arithmetic: 3.27 us -> 6.1 us
    dot_general x4 -> x0, matrix products: 59.2 us -> none  [the longest x1 21.2 us: local(): jnp.einsum('brc,bcd->brd', a_blocks, col_onehot, precision=lax.Precision....]
    reduce_scatter x1 -> x0, waiting for transfers between devices: 24.5 us -> none  [local(): lax.psum_scatter(partial_value, 'narrow', scatter_dimension=1, tiled=True)]
    unnamed x2 -> x0, blocking collectives: 19.8 us -> none
    ppermute x0 -> x9, waiting for transfers between devices: none -> 18.7 us  [exchange(): return lax.ppermute(x, axis, [(i, i ^ bit) for i in range(size)])]
    all_gather x1 -> x0, waiting for transfers between devices: 14.4 us -> none  [local(): blocks_in = lax.all_gather(accumulated_sum, 'wide', axis=0, tiled=True)]
    ppermute x0 -> x9, starting transfers between devices: none -> 13.6 us  [exchange(): return lax.ppermute(x, axis, [(i, i ^ bit) for i in range(size)])]
    pallas_call x0 -> x1, Pallas kernels: none -> 11.1 us  [coarsen(): pl.pallas_call(functools.partial(coarsen_body, places=places, rows=rows),...]
    select_n x1 -> x7, other arithmetic: 0.13 us -> 2.87 us  [the longest x1 1.38 us: local(): slot_of = target % counts[0]]
  transfers between devices with their start and end apart: 2 -> 9, of which waited for: 2 -> 6; matrix products, arithmetic and copies ran while one was open for 3% -> 10% of each run, Pallas kernels for 0% -> 21%
where the time goes in v1:
time: 53.1 us; the launch traced here: 52.9 us
  waiting for transfers between devices  18.7 us (35%)
  starting transfers between devices  13.6 us (26%)
  Pallas kernels  11.1 us (21%)
  other arithmetic  6.1 us (11%)
  local copies, waits for them, and re-layouts  1.95 us (4%)
  between operations  1.52 us (3%)
    ppermute x9, waiting for transfers between devices, exchange(): return lax.ppermute(x, axis, [(i, i ^ bit) for i in range(size)])  18.7 us
    ppermute x9, starting transfers between devices, exchange(): return lax.ppermute(x, axis, [(i, i ^ bit) for i in range(size)])  13.6 us
    pallas_call x1, Pallas kernels, coarsen(): pl.pallas_call(functools.partial(coarsen_body, places=places, rows=rows),...  11.1 us
    add x2, other arithmetic, local(): piece[rel ^ 1 << k] + exchange(piece[rel], 'narrow', 1 << k)  1.86 us
    select_n x1, other arithmetic, local(): slot_of = target % counts[0]  1.38 us
  transfers between devices with their start and end apart: 9, of which 6 were waited for; matrix products, arithmetic and copies ran while one was open for 10% of the time, Pallas kernels for 21%

profile of v1, /device:TPU:0, one launch (start us, length us, event | category | flops | bytes accessed | tf_op | source)
XLA Modules:
  0.0 52.9 jit_solution(6673007669286744043)
XLA Ops:
  1.3 0.7 %add_bitcast_fusion = s32[1,9]{1,0:T(1,128)S(1)} fusion(s32[8]{0:T(128)} %param.11, s32[1]{0:T(128)} %copy.8), kind=kLoop, calls=%fused_computation.37 | loop fusion | flops 9 | bytes 72 | tf_op jit(solution)/shard_map/broadcast_in_dim | solution.py:94
  2.0 3.0 %collective-permute-start = (s32[1,9]{1,0:T(1,128)S(1)}, s32[1,9]{1,0:T(1,128)S(1)}, u32[]{:S(2)}, u32[]{:S(2)}) collective-permute-start(s32[1,9]{1,0:T(1,128)S(1)} %add_bitcast_fusion), channel_id=1, source_target_pairs={{0,4},{4,0},{8,12},{12,8},{16,20},{20,16},{24,28},{28,24},{1,5},{5... | collective-permute-start | bytes 116 | tf_op jit(solution)/shard_map/ppermute | solution.py:83
  5.0 1.4 %and_select_fusion.slot_ref = s32[192]{0:T(256)} fusion(s32[192]{0:T(256)} %param.9, pred[]{:T(512)S(6)} %lt.77, s32[]{:T(128)S(6)} %select_n.113), kind=kLoop, calls=%fused_computation.27 | loop fusion | flops 1344 | bytes 1541 | tf_op jit(solution)/shard_map/jit(remainder)/select_n | solution.py:98
  6.4 11.1 %coarsen.1 = (f32[2,8,32,128]{3,2,1,0:T(8,128)}, f32[1,8,32,128]{3,2,1,0:T(8,128)}, f32[1,8,32,128]{3,2,1,0:T(8,128)}) custom-call(s32[192]{0:T(256)} %and_select_fusion.slot_ref, s32[1]{0:T(128)} %bitcast.2.me_ref, f32[192,128,128]{2,1,0:T(8,128)} %a_ref.1, s32[192,128]{1,0:T(8,128)} %row_ref.1, s32[192,128]{1,0:T(8,128)} %col_ref.1), custom_call_target="tpu_custom_call" | custom-call | flops 3221225472 | bytes 12582912 | tf_op jit(solution)/shard_map/coarsen/pallas_call | solution.py:60
  17.4 1.0 %slice_bitcast_fusion.1 = (f32[8,32,128]{2,1,0:T(8,128)S(1)}, f32[8,32,128]{2,1,0:T(8,128)S(1)}) fusion(f32[2,8,32,128]{3,2,1,0:T(8,128)} %get-tuple-element.6), kind=kLoop, calls=%fused_computation.8 | loop fusion | bytes 524288 | tf_op jit(solution)/shard_map/unstack | solution.py:125
  18.4 0.1 collective-permute-start.3
  18.5 0.5 collective-permute-start.4
  19.0 0.1 ge.43
  19.1 0.1 ne.114
  19.2 0.1 ge.42
  19.3 0.1 and.228
  19.3 0.0 collective-permute-done
  19.4 1.6 %collective-permute-start.1 = (s32[2,9]{1,0:T(2,128)S(1)}, s32[2,9]{1,0:T(2,128)S(1)}, u32[]{:S(2)}, u32[]{:S(2)}) collective-permute-start(s32[2,9]{1,0:T(2,128)S(1)} %pad_add_fusion.2), channel_id=1, source_target_pairs={{0,8},{4,12},{8,0},{12,4},{16,24},{20,28},{24,16},{28,20},{1,9},{5... | collective-permute-start | bytes 224 | tf_op jit(solution)/shard_map/ppermute | solution.py:83
  21.0 0.1 ge.40
  21.1 0.1 and.215
  21.2 1.8 %collective-permute-done.1 = s32[2,9]{1,0:T(2,128)S(1)} collective-permute-done((s32[2,9]{1,0:T(2,128)S(1)}, s32[2,9]{1,0:T(2,128)S(1)}, u32[]{:S(2)}, u32[]{:S(2)}) %collective-permute-start.1) | collective-permute-done | bytes 104 | tf_op jit(solution)/shard_map/ppermute | solution.py:83
  23.0 2.7 %collective-permute-start.2 = (s32[4,9]{1,0:T(4,128)S(1)}, s32[4,9]{1,0:T(4,128)S(1)}, u32[]{:S(2)}, u32[]{:S(2)}) collective-permute-start(s32[4,9]{1,0:T(4,128)S(1)} %pad_add_fusion.1), channel_id=1, source_target_pairs={{0,16},{4,20},{8,24},{12,28},{16,0},{20,4},{24,8},{28,12},{1,17},{... | collective-permute-start | bytes 440 | tf_op jit(solution)/shard_map/ppermute | solution.py:83
  25.7 0.1 ge.41
  25.7 0.1 and.220
  25.8 1.7 %collective-permute-done.2 = s32[4,9]{1,0:T(4,128)S(1)} collective-permute-done((s32[4,9]{1,0:T(4,128)S(1)}, s32[4,9]{1,0:T(4,128)S(1)}, u32[]{:S(2)}, u32[]{:S(2)}) %collective-permute-start.2) | collective-permute-done | bytes 176 | tf_op jit(solution)/shard_map/ppermute | solution.py:83
  27.6 0.1 slice_reduce_fusion
  27.7 0.2 select_reduce_fusion.1
  28.0 0.1 add_select_fusion
  28.1 0.1 select_n.110
  28.2 0.0 collective-permute-done.4
  28.2 0.9 %bitcast_add_fusion = f32[8,32,128]{2,1,0:T(8,128)S(1)} fusion(f32[8,32,128]{2,1,0:T(8,128)S(1)} %collective-permute-done.4, f32[1,8,32,128]{3,2,1,0:T(8,128)} %get-tuple-element.7), kind=kLoop, calls=%fused_computation.3 | loop fusion | flops 32768 | bytes 393216 | tf_op jit(solution)/shard_map/add | solution.py:135
  29.1 1.6 %collective-permute-start.5 = (f32[8,32,128]{2,1,0:T(8,128)S(1)}, f32[8,32,128]{2,1,0:T(8,128)S(1)}, u32[]{:S(2)}, u32[]{:S(2)}) collective-permute-start(f32[8,32,128]{2,1,0:T(8,128)S(1)} %bitcast_add_fusion), channel_id=1, source_target_pairs={{0,2},{1,3},{2,0},{3,1},{4,6},{5,7},{6,4},{7,5},{8,10},{9,11},{10,... | collective-permute-start | bytes 393224 | tf_op jit(solution)/shard_map/ppermute | solution.py:83
  30.7 0.0 collective-permute-done.3
  30.8 3.4 %collective-permute-done.5 = f32[8,32,128]{2,1,0:T(8,128)S(1)} collective-permute-done((f32[8,32,128]{2,1,0:T(8,128)S(1)}, f32[8,32,128]{2,1,0:T(8,128)S(1)}, u32[]{:S(2)}, u32[]{:S(2)}) %collective-permute-start.5) | collective-permute-done | bytes 131104 | tf_op jit(solution)/shard_map/ppermute | solution.py:83
  34.2 0.9 %fusion.1 = f32[8,32,128]{2,1,0:T(8,128)S(1)} fusion(f32[8,32,128]{2,1,0:T(8,128)S(1)} %collective-permute-done.5, f32[8,32,128]{2,1,0:T(8,128)S(1)} %collective-permute-done.3, f32[1,8,32,128]{3,2,1,0:T(8,128)} %get-tuple-element.5), kind=kLoop, calls=%fused_computation.5 | loop fusion | flops 65536 | bytes 524288 | tf_op jit(solution)/shard_map/add | solution.py:135
  35.2 0.3 collective-permute-start.6
  35.4 0.1 fusion.6
  35.6 4.6 %collective-permute-done.6 = f32[8,32,128]{2,1,0:T(8,128)S(1)} collective-permute-done((f32[8,32,128]{2,1,0:T(8,128)S(1)}, f32[8,32,128]{2,1,0:T(8,128)S(1)}, u32[]{:S(2)}, u32[]{:S(2)}) %collective-permute-start.6) | collective-permute-done | bytes 131104 | tf_op jit(solution)/shard_map/ppermute | solution.py:83
  40.2 0.1 broadcast_select_fusion
  40.3 1.6 %collective-permute-start.7 = (f32[8,32,128]{2,1,0:T(8,128)S(1)}, f32[8,32,128]{2,1,0:T(8,128)S(1)}, u32[]{:S(2)}, u32[]{:S(2)}) collective-permute-start(f32[8,32,128]{2,1,0:T(8,128)S(1)} %broadcast_select_fusion), channel_id=1, source_target_pairs={{0,8},{4,12},{8,0},{12,4},{16,24},{20,28},{24,16},{28,20},{1,9},{5... | collective-permute-start | bytes 393224 | tf_op jit(solution)/shard_map/ppermute | solution.py:83
  41.9 0.1 slice.11
  42.0 0.1 broadcast_in_dim.103
  42.1 0.2 select_reduce_fusion
  42.3 3.9 %collective-permute-done.7 = f32[8,32,128]{2,1,0:T(8,128)S(1)} collective-permute-done((f32[8,32,128]{2,1,0:T(8,128)S(1)}, f32[8,32,128]{2,1,0:T(8,128)S(1)}, u32[]{:S(2)}, u32[]{:S(2)}) %collective-permute-start.7) | collective-permute-done | bytes 131104 | tf_op jit(solution)/shard_map/ppermute | solution.py:83
  46.2 0.1 broadcast_select_fusion.1
  46.2 2.2 %collective-permute-start.8 = (f32[8,32,128]{2,1,0:T(8,128)S(1)}, f32[8,32,128]{2,1,0:T(8,128)S(1)}, u32[]{:S(2)}, u32[]{:S(2)}) collective-permute-start(f32[8,32,128]{2,1,0:T(8,128)S(1)} %broadcast_select_fusion.1), channel_id=1, source_target_pairs={{0,16},{4,20},{8,24},{12,28},{16,0},{20,4},{24,8},{28,12},{1,17},{... | collective-permute-start | bytes 393224 | tf_op jit(solution)/shard_map/ppermute | solution.py:83
  48.5 0.5 broadcast_select_fusion.2
  49.0 3.2 %collective-permute-done.8 = f32[8,32,128]{2,1,0:T(8,128)S(1)} collective-permute-done((f32[8,32,128]{2,1,0:T(8,128)S(1)}, f32[8,32,128]{2,1,0:T(8,128)S(1)}, u32[]{:S(2)}, u32[]{:S(2)}) %collective-permute-start.8) | collective-permute-done | bytes 131104 | tf_op jit(solution)/shard_map/ppermute | solution.py:83
  52.2 0.7 %select_select_fusion = f32[8,32,128]{2,1,0:T(8,128)} fusion(f32[8,32,128]{2,1,0:T(8,128)S(1)} %collective-permute-done.8, f32[8,32,128]{2,1,0:T(8,128)S(1)} %broadcast_select_fusion.1, pred[8]{0:T(512)(128)(4,1)S(1)} %get-tuple-element.11, pred[8]{0:T(512)(128)(4,1)S(1)} %get-tuple-element.8), kind=kLoop, calls=%fused_computation.6 | loop fusion | flops 65536 | bytes 393232 | tf_op jit(solution)/shard_map/jit(_where)/select_n | solution.py:141
  (13 shorter events, 0.1 us)
Async XLA Ops:
  2.0 17.3 %collective-permute-start = (s32[1,9]{1,0:T(1,128)S(1)}, s32[1,9]{1,0:T(1,128)S(1)}, u32[]{:S(2)}, u32[]{:S(2)}) collective-permute-start(s32[1,9]{1,0:T(1,128)S(1)} %add_bitcast_fusion), channel_id=1, source_target_pairs={{0,4},{4,0},{8,12},{12,8},{16,20},{20,16},{24,28},{28,24},{1,5},{5... | collective-permute-start | bytes 116 | tf_op jit(solution)/shard_map/ppermute | solution.py:83
  18.4 12.3 %collective-permute-start.3 = (f32[8,32,128]{2,1,0:T(8,128)S(1)}, f32[8,32,128]{2,1,0:T(8,128)S(1)}, u32[]{:S(2)}, u32[]{:S(2)}) collective-permute-start(f32[8,32,128]{2,1,0:T(8,128)S(1)} %get-tuple-element.14), channel_id=1, source_target_pairs={{0,1},{1,0},{2,3},{3,2},{4,5},{5,4},{6,7},{7,6},{8,9},{9,8},{10,11... | collective-permute-start | bytes 393224 | tf_op jit(solution)/shard_map/ppermute | solution.py:83
  18.5 9.7 %collective-permute-start.4 = (f32[8,32,128]{2,1,0:T(8,128)S(1)}, f32[8,32,128]{2,1,0:T(8,128)S(1)}, u32[]{:S(2)}, u32[]{:S(2)}) collective-permute-start(f32[8,32,128]{2,1,0:T(8,128)S(1)} %get-tuple-element.15), channel_id=1, source_target_pairs={{0,1},{1,0},{2,3},{3,2},{4,5},{5,4},{6,7},{7,6},{8,9},{9,8},{10,11... | collective-permute-start | bytes 393224 | tf_op jit(solution)/shard_map/ppermute | solution.py:83
  19.4 3.6 %collective-permute-start.1 = (s32[2,9]{1,0:T(2,128)S(1)}, s32[2,9]{1,0:T(2,128)S(1)}, u32[]{:S(2)}, u32[]{:S(2)}) collective-permute-start(s32[2,9]{1,0:T(2,128)S(1)} %pad_add_fusion.2), channel_id=1, source_target_pairs={{0,8},{4,12},{8,0},{12,4},{16,24},{20,28},{24,16},{28,20},{1,9},{5... | collective-permute-start | bytes 224 | tf_op jit(solution)/shard_map/ppermute | solution.py:83
  23.0 4.5 %collective-permute-start.2 = (s32[4,9]{1,0:T(4,128)S(1)}, s32[4,9]{1,0:T(4,128)S(1)}, u32[]{:S(2)}, u32[]{:S(2)}) collective-permute-start(s32[4,9]{1,0:T(4,128)S(1)} %pad_add_fusion.1), channel_id=1, source_target_pairs={{0,16},{4,20},{8,24},{12,28},{16,0},{20,4},{24,8},{28,12},{1,17},{... | collective-permute-start | bytes 440 | tf_op jit(solution)/shard_map/ppermute | solution.py:83
  29.1 5.0 %collective-permute-start.5 = (f32[8,32,128]{2,1,0:T(8,128)S(1)}, f32[8,32,128]{2,1,0:T(8,128)S(1)}, u32[]{:S(2)}, u32[]{:S(2)}) collective-permute-start(f32[8,32,128]{2,1,0:T(8,128)S(1)} %bitcast_add_fusion), channel_id=1, source_target_pairs={{0,2},{1,3},{2,0},{3,1},{4,6},{5,7},{6,4},{7,5},{8,10},{9,11},{10,... | collective-permute-start | bytes 393224 | tf_op jit(solution)/shard_map/ppermute | solution.py:83
  35.2 5.0 %collective-permute-start.6 = (f32[8,32,128]{2,1,0:T(8,128)S(1)}, f32[8,32,128]{2,1,0:T(8,128)S(1)}, u32[]{:S(2)}, u32[]{:S(2)}) collective-permute-start(f32[8,32,128]{2,1,0:T(8,128)S(1)} %fusion), channel_id=1, source_target_pairs={{0,4},{4,0},{8,12},{12,8},{16,20},{20,16},{24,28},{28,24},{1,5},{5... | collective-permute-start | bytes 393224 | tf_op jit(solution)/shard_map/ppermute | solution.py:83
  40.3 5.9 %collective-permute-start.7 = (f32[8,32,128]{2,1,0:T(8,128)S(1)}, f32[8,32,128]{2,1,0:T(8,128)S(1)}, u32[]{:S(2)}, u32[]{:S(2)}) collective-permute-start(f32[8,32,128]{2,1,0:T(8,128)S(1)} %broadcast_select_fusion), channel_id=1, source_target_pairs={{0,8},{4,12},{8,0},{12,4},{16,24},{20,28},{24,16},{28,20},{1,9},{5... | collective-permute-start | bytes 393224 | tf_op jit(solution)/shard_map/ppermute | solution.py:83
  46.2 5.9 %collective-permute-start.8 = (f32[8,32,128]{2,1,0:T(8,128)S(1)}, f32[8,32,128]{2,1,0:T(8,128)S(1)}, u32[]{:S(2)}, u32[]{:S(2)}) collective-permute-start(f32[8,32,128]{2,1,0:T(8,128)S(1)} %broadcast_select_fusion.1), channel_id=1, source_target_pairs={{0,16},{4,20},{8,24},{12,28},{16,0},{20,4},{24,8},{28,12},{1,17},{... | collective-permute-start | bytes 393224 | tf_op jit(solution)/shard_map/ppermute | solution.py:83

commit v2 on v0

v2 whole, which is shorter than its diff:
```python
import functools

import jax
import jax.numpy as jnp
from jax import lax
from jax.experimental import pallas as pl
from jax.experimental.pallas import tpu as pltpu
from jax.sharding import PartitionSpec as P


F32, BF16 = jnp.float32, jnp.bfloat16
NT = (((1,), (1,)), ((), ()))
GROUP = 32


def split(a):
    hi = a.astype(BF16)
    return hi, (a - hi.astype(F32)).astype(BF16)


def onehot(vec, pos):
    return jnp.where(vec.astype(F32).astype(BF16) == pos, jnp.ones((), BF16), jnp.zeros((), BF16))


def coarsen_body(
    count_ref, weight_hbm, target_hbm, a_hbm, row_hbm, col_hbm, table_out, *refs, group, piece, axis
):
    outs, refs = refs[:-8], refs[-8:]
    weight_ref, target_ref, row_ref, col_ref, a_buf, y_buf, sems, small_sems = refs
    parts = len(outs)
    count, n, _ = a_buf.shape
    rows = n // parts
    chunks, per = count // group, group // piece
    me = lax.axis_index(axis)

    def copy(k):
        at = pl.ds(k * piece, piece)
        return pltpu.make_async_copy(a_hbm.at[at], a_buf.at[at], sems.at[k])

    small = [
        pltpu.make_async_copy(src, dst, small_sems.at[k])
        for k, (src, dst) in enumerate(
            (
                (row_hbm, row_ref),
                (weight_hbm, weight_ref),
                (target_hbm, target_ref),
                (col_hbm, col_ref),
            )
        )
    ]
    small[0].start()
    copy(0).start()
    for c in small[1:]:
        c.start()
    for k in range(1, min(2, chunks) * per):
        copy(k).start()
    for o in outs:
        o[...] = jnp.zeros_like(o)
    iota = lax.broadcasted_iota(jnp.int32, (n, n), 0)
    row_pos = (((iota // rows) ^ me) * rows + iota % rows).astype(F32).astype(BF16)
    col_pos = iota.astype(F32).astype(BF16)

    for c in small:
        c.wait()
    live = count_ref[0]
    lane = lax.broadcasted_iota(jnp.int32, table_out.shape, 1)
    table = jnp.where(lane == 0, live, 0)
    for k in range(weight_ref.shape[0]):
        table = jnp.where(lane == k + 1, weight_ref[k], table)
    table_out[...] = table
    inverse = 65536 // live + 1

    def rows_step(block, row_vec, g):
        r = onehot(row_vec, row_pos)
        y = jnp.dot(
            jnp.concatenate([r, r], 1), jnp.concatenate(split(a_buf[block]), 0), preferred_element_type=F32
        )
        hi, lo = split(y)
        y_buf[g, :, :n] = hi
        y_buf[g, :, n:] = lo

    def cols_step(block, col_vec, g):
        c = onehot(col_vec, col_pos)
        x = lax.dot_general(y_buf[g], jnp.concatenate([c, c], 1), NT, preferred_element_type=F32)
        t = target_ref[block]
        s = t - ((t * inverse) >> 16) * live
        for rel, o in enumerate(outs):
            o[s] += x[rel * rows : (rel + 1) * rows]

    def vectors(ref, i):
        return ref[pl.ds(pl.multiple_of(i * group, 8), group), :]

    first = row_ref[:group, :]
    for g in range(group):
        if g % piece == 0:
            copy(g // piece).wait()
        rows_step(g, first[g : g + 1], g)

    def step(i, carry):
        for k in range(per):
            copy(i * per + k).wait()

        @pl.when(i + 1 < chunks)
        def _():
            for k in range(per):
                copy((i + 1) * per + k).start()

        row_vecs, col_vecs = vectors(row_ref, i), vectors(col_ref, i - 1)
        for g in range(group):
            cols_step((i - 1) * group + g, col_vecs[g : g + 1], g)
            rows_step(i * group + g, row_vecs[g : g + 1], g)
        return carry

    lax.fori_loop(1, chunks, step, 0)
    last = vectors(col_ref, chunks - 1)
    for g in range(group):
        cols_step((chunks - 1) * group + g, last[g : g + 1], g)


def coarsen(counts, weights, target, a_blocks, row_map, col_map, parts, axis):
    args = (weights, target, a_blocks, row_map, col_map)
    slots = weights.shape[0]
    width = pl.cdiv(slots + 1, 128) * 128
    count, n, _ = a_blocks.shape
    rows = n // parts
    piece = 8
    group = max(g for g in range(piece, GROUP + 1, piece) if count % g == 0)
    hbm = pl.BlockSpec(memory_space=pltpu.HBM)
    vmem = pl.BlockSpec(memory_space=pltpu.VMEM)
    return pl.pallas_call(
        functools.partial(coarsen_body, group=group, piece=piece, axis=axis),
        out_shape=[jax.ShapeDtypeStruct((1, width), jnp.int32)]
        + [jax.ShapeDtypeStruct((slots, rows, n), F32) for _ in range(parts)],
        in_specs=[pl.BlockSpec(memory_space=pltpu.SMEM)] + [hbm] * len(args),
        out_specs=[vmem] * (parts + 1),
        scratch_shapes=[
            pltpu.SMEM(weights.shape, jnp.int32),
            pltpu.SMEM(target.shape, jnp.int32),
            pltpu.VMEM(row_map.shape, jnp.int32),
            pltpu.VMEM(col_map.shape, jnp.int32),
            pltpu.VMEM((count, n, n), F32),
            pltpu.VMEM((group, n, 2 * n), BF16),
            pltpu.SemaphoreType.DMA((count // piece,)),
            pltpu.SemaphoreType.DMA((4,)),
        ],
        compiler_params=pltpu.CompilerParams(vmem_limit_bytes=24 << 20),
        cost_estimate=pl.CostEstimate(
            flops=count * 8 * n**3, bytes_accessed=count * n * n * 4, transcendentals=0
        ),
        name="coarsen",
    )(counts, *(pltpu.with_memory_space_constraint(x, pltpu.HBM) for x in args))


def exchange(x, axis, bit):
    size = lax.axis_size(axis)
    return lax.ppermute(x, axis, [(i, i ^ bit) for i in range(size)])


def local(a_blocks, row_map, col_map, target, counts, weights):
    slots = weights.shape[0]
    parts = lax.axis_size("narrow")
    nwide = lax.axis_size("wide")
    own = lax.axis_index("wide")
    bits = [1 << k for k in range(nwide.bit_length() - 1)]
    lane_bits = [1 << k for k in range(slots.bit_length() - 1)]
    assert slots & (slots - 1) == 0 and nwide & (nwide - 1) == 0 and parts & (parts - 1) == 0

    table, *outs = coarsen(counts, weights, target, a_blocks, row_map, col_map, parts, "narrow")

    for bit in bits:
        table = jnp.concatenate([table, exchange(table, "wide", bit)], 0)

    piece = list(outs)
    for k in range(parts.bit_length() - 1):
        for rel in reversed([r for r in range(parts) if r and (r & -r) == 1 << k]):
            other = exchange(piece[rel], "narrow", 1 << k)
            piece[rel ^ (1 << k)] = piece[rel ^ (1 << k)] + other
    value = piece[0]

    count_of = table[:, 0]
    owner = own ^ jnp.arange(nwide, dtype=jnp.int32)
    later = owner[None, :] >= owner[:, None]
    start = nwide * slots - jnp.sum(jnp.where(later, count_of[None, :], 0), 1)
    slot = jnp.arange(slots, dtype=jnp.int32)
    live = slot[None, :] < count_of[:, None]
    origin = (owner[:, None] * slots + slot[None, :]).reshape(-1)
    place = jnp.where(live, start[:, None] + slot[None, :], -1).reshape(-1)
    weight_of = table[:, 1 : slots + 1].reshape(-1)

    def holds(index, device, such):
        here = index[None, :] == (device * slots + slot)[:, None]
        return jnp.any(here & such[None, :], 1)[:, None, None]

    def take(bit, device):
        before = (origin & -bit) | (place & (bit - 1))
        after = (origin & (-2 * bit)) | (place & (2 * bit - 1))
        return holds(after, device, (place >= 0) & (after != before))

    def turned(x, device):
        for bit in lane_bits:
            pairs = x.reshape(slots // (2 * bit), 2, bit, *x.shape[1:])
            x = jnp.where(take(bit, device), jnp.flip(pairs, 1).reshape(x.shape), x)
        return x

    for bit in bits:
        other = exchange(value, "wide", bit)
        if bit == 1:
            value, other = turned(value, own), turned(other, own ^ bit)
        value = jnp.where(take(bit * slots, own), other, value)
    valid = holds(place, own, place >= 0)
    value = jnp.where(valid, value, 0.0)
    above = place[None, :] > (own * slots + slot)[:, None]
    offset = jnp.where(valid[:, 0, 0], jnp.sum(jnp.where(above, weight_of[None, :], 0), 1), 0)
    return value, offset.astype(jnp.int32)


def solution(mesh):
    return jax.shard_map(
        local,
        mesh=mesh,
        in_specs=(
            P(("wide", "narrow"), None, None),
            P(("wide", "narrow"), None),
            P(("wide", "narrow"), None),
            P(("wide", "narrow")),
            P("wide"),
            P("wide"),
        ),
        out_specs=(P("wide", "narrow", None), P("wide")),
        check_vma=False,
    )
```

time: 141 us -> 49.8 us (0.35)
  matrix products: 59.2 us -> 0 us
  waiting for transfers between devices: 38.9 us -> 15.7 us
  blocking collectives: 19.8 us -> 0 us
  starting transfers between devices: 0.08 us -> 17.6 us
  between operations: 17.9 us -> 1.4 us
  Pallas kernels: 0 us -> 11.5 us
    dot_general x4 -> x0, matrix products: 59.2 us -> none  [the longest x1 21.2 us: local(): jnp.einsum('brc,bcd->brd', a_blocks, col_onehot, precision=lax.Precision....]
    reduce_scatter x1 -> x0, waiting for transfers between devices: 24.5 us -> none  [local(): lax.psum_scatter(partial_value, 'narrow', scatter_dimension=1, tiled=True)]
    unnamed x2 -> x0, blocking collectives: 19.8 us -> none
    ppermute x0 -> x9, starting transfers between devices: none -> 17.6 us  [exchange(): return lax.ppermute(x, axis, [(i, i ^ bit) for i in range(size)])]
    ppermute x0 -> x9, waiting for transfers between devices: none -> 15.7 us  [exchange(): return lax.ppermute(x, axis, [(i, i ^ bit) for i in range(size)])]
    all_gather x1 -> x0, waiting for transfers between devices: 14.4 us -> none  [local(): blocks_in = lax.all_gather(accumulated_sum, 'wide', axis=0, tiled=True)]
    pallas_call x0 -> x1, Pallas kernels: none -> 11.5 us  [coarsen(): pl.pallas_call(functools.partial(coarsen_body, group=group, piece=piece,...]
    select_n x1 -> x9, other arithmetic: 0.13 us -> 1.83 us  [the longest x1 0.74 us: local(): value = jnp.where(valid, value, 0.0)]
  transfers between devices with their start and end apart: 2 -> 9, of which waited for: 2 -> 7; matrix products, arithmetic and copies ran while one was open for 3% -> 4% of each run, Pallas kernels for 0% -> 0%
where the time goes in v2:
time: 49.8 us; the launch traced here: 49.4 us
  starting transfers between devices  17.6 us (35%)
  waiting for transfers between devices  15.7 us (32%)
  Pallas kernels  11.5 us (23%)
  other arithmetic  2.73 us (5%)
  between operations  1.4 us (3%)
    ppermute x9, starting transfers between devices, exchange(): return lax.ppermute(x, axis, [(i, i ^ bit) for i in range(size)])  17.6 us
    ppermute x9, waiting for transfers between devices, exchange(): return lax.ppermute(x, axis, [(i, i ^ bit) for i in range(size)])  15.7 us
    pallas_call x1, Pallas kernels, coarsen(): pl.pallas_call(functools.partial(coarsen_body, group=group, piece=piece,...  11.5 us
  transfers between devices with their start and end apart: 9, of which 7 were waited for; matrix products, arithmetic and copies ran while one was open for 4% of the time, Pallas kernels for 0%

profile of v2, /device:TPU:0, one launch (start us, length us, event | category | flops | bytes accessed | tf_op | source)
XLA Modules:
  0.0 49.4 jit_solution(17129879280511618063)
XLA Ops:
  1.3 11.5 %coarsen.1 = (s32[1,128]{1,0:T(1,128)S(1)}, f32[8,32,128]{2,1,0:T(8,128)S(1)}, f32[8,32,128]{2,1,0:T(8,128)S(1)}, f32[8,32,128]{2,1,0:T(8,128)S(1)}, f32[8,32,128]{2,1,0:T(8,128)S(1)}) custom-call(s32[1]{0:T(128)S(6)} %copy.8.count_ref, s32[8]{0:T(128)} %weight_hbm.1, s32[192]{0:T(256)} %target_hbm.1, f32[192,128,128]{2,1,0:T(8,128)} %a_hbm.1, ...), custom_call_target="tpu_custom_call" | custom-call | flops 3221225472 | bytes 12582912 | tf_op jit(solution)/shard_map/coarsen/pallas_call | solution.py:130
  12.8 0.5 %collective-permute-start.4 = (f32[8,32,128]{2,1,0:T(8,128)S(1)}, f32[8,32,128]{2,1,0:T(8,128)S(1)}, u32[]{:S(2)}, u32[]{:S(2)}) collective-permute-start(f32[8,32,128]{2,1,0:T(8,128)S(1)} %get-tuple-element.11), channel_id=1, source_target_pairs={{0,1},{1,0},{2,3},{3,2},{4,5},{5,4},{6,7},{7,6},{8,9},{9,8},{10,11... | collective-permute-start | bytes 393224 | tf_op jit(solution)/shard_map/ppermute | solution.py:156
  13.3 0.1 collective-permute-start.3
  13.4 2.9 %collective-permute-start = (s32[1,128]{1,0:T(1,128)S(1)}, s32[1,128]{1,0:T(1,128)S(1)}, u32[]{:S(2)}, u32[]{:S(2)}) collective-permute-start(s32[1,128]{1,0:T(1,128)S(1)} %get-tuple-element.7), channel_id=1, source_target_pairs={{0,4},{4,0},{8,12},{12,8},{16,20},{20,16},{24,28},{28,24},{1,5},{5... | collective-permute-start | bytes 1544 | tf_op jit(solution)/shard_map/ppermute | solution.py:156
  16.4 0.1 iota_add_fusion
  16.4 1.5 %collective-permute-done = s32[1,128]{1,0:T(1,128)S(1)} collective-permute-done((s32[1,128]{1,0:T(1,128)S(1)}, s32[1,128]{1,0:T(1,128)S(1)}, u32[]{:S(2)}, u32[]{:S(2)}) %collective-permute-start) | collective-permute-done | bytes 544 | tf_op jit(solution)/shard_map/ppermute | solution.py:156
  17.9 2.1 %collective-permute-start.1 = (s32[2,128]{1,0:T(2,128)S(1)}, s32[2,128]{1,0:T(2,128)S(1)}, u32[]{:S(2)}, u32[]{:S(2)}) collective-permute-start(s32[2,128]{1,0:T(2,128)S(1)} %pad_add_fusion.2), channel_id=1, source_target_pairs={{0,8},{4,12},{8,0},{12,4},{16,24},{20,28},{24,16},{28,20},{1,9},{5... | collective-permute-start | bytes 3080 | tf_op jit(solution)/shard_map/ppermute | solution.py:156
  20.1 1.5 %collective-permute-done.1 = s32[2,128]{1,0:T(2,128)S(1)} collective-permute-done((s32[2,128]{1,0:T(2,128)S(1)}, s32[2,128]{1,0:T(2,128)S(1)}, u32[]{:S(2)}, u32[]{:S(2)}) %collective-permute-start.1) | collective-permute-done | bytes 1056 | tf_op jit(solution)/shard_map/ppermute | solution.py:156
  21.6 3.1 %collective-permute-start.2 = (s32[4,128]{1,0:T(4,128)S(1)}, s32[4,128]{1,0:T(4,128)S(1)}, u32[]{:S(2)}, u32[]{:S(2)}) collective-permute-start(s32[4,128]{1,0:T(4,128)S(1)} %pad_add_fusion.1), channel_id=1, source_target_pairs={{0,16},{4,20},{8,24},{12,28},{16,0},{20,4},{24,8},{28,12},{1,17},{... | collective-permute-start | bytes 6152 | tf_op jit(solution)/shard_map/ppermute | solution.py:156
  24.7 0.1 add.161
  24.8 1.5 %collective-permute-done.2 = s32[4,128]{1,0:T(4,128)S(1)} collective-permute-done((s32[4,128]{1,0:T(4,128)S(1)}, s32[4,128]{1,0:T(4,128)S(1)}, u32[]{:S(2)}, u32[]{:S(2)}) %collective-permute-start.2) | collective-permute-done | bytes 2080 | tf_op jit(solution)/shard_map/ppermute | solution.py:156
  26.3 0.1 slice_reduce_fusion
  26.4 0.2 select_reduce_fusion.1
  26.6 0.1 add_select_fusion
  26.7 0.1 select_n.97
  26.8 0.0 collective-permute-done.4
  26.8 1.9 %collective-permute-start.5 = (f32[8,32,128]{2,1,0:T(8,128)S(1)}, f32[8,32,128]{2,1,0:T(8,128)S(1)}, u32[]{:S(2)}, u32[]{:S(2)}) collective-permute-start(f32[8,32,128]{2,1,0:T(8,128)S(1)} %add.165), channel_id=1, source_target_pairs={{0,2},{1,3},{2,0},{3,1},{4,6},{5,7},{6,4},{7,5},{8,10},{9,11},{10,... | collective-permute-start | bytes 393224 | tf_op jit(solution)/shard_map/ppermute | solution.py:156
  28.7 0.3 and_reduce_fusion.3
  29.0 0.0 collective-permute-done.3
  29.0 2.8 %collective-permute-done.5 = f32[8,32,128]{2,1,0:T(8,128)S(1)} collective-permute-done((f32[8,32,128]{2,1,0:T(8,128)S(1)}, f32[8,32,128]{2,1,0:T(8,128)S(1)}, u32[]{:S(2)}, u32[]{:S(2)}) %collective-permute-start.5) | collective-permute-done | bytes 131104 | tf_op jit(solution)/shard_map/ppermute | solution.py:156
  31.9 1.9 %collective-permute-start.6 = (f32[8,32,128]{2,1,0:T(8,128)S(1)}, f32[8,32,128]{2,1,0:T(8,128)S(1)}, u32[]{:S(2)}, u32[]{:S(2)}) collective-permute-start(f32[8,32,128]{2,1,0:T(8,128)S(1)} %add_add_fusion), channel_id=1, source_target_pairs={{0,4},{4,0},{8,12},{12,8},{16,20},{20,16},{24,28},{28,24},{1,5},{5... | collective-permute-start | bytes 393224 | tf_op jit(solution)/shard_map/ppermute | solution.py:156
  33.8 0.1 bitcast_select_fusion.2
  33.9 0.1 bitcast_select_fusion.1
  34.0 3.0 %collective-permute-done.6 = f32[8,32,128]{2,1,0:T(8,128)S(1)} collective-permute-done((f32[8,32,128]{2,1,0:T(8,128)S(1)}, f32[8,32,128]{2,1,0:T(8,128)S(1)}, u32[]{:S(2)}, u32[]{:S(2)}) %collective-permute-start.6) | collective-permute-done | bytes 131104 | tf_op jit(solution)/shard_map/ppermute | solution.py:156
  36.9 0.1 bitcast_select_fusion.5
  37.0 0.1 bitcast_select_fusion.4
  37.1 0.1 fusion
  37.3 2.0 %collective-permute-start.7 = (f32[8,32,128]{2,1,0:T(8,128)S(1)}, f32[8,32,128]{2,1,0:T(8,128)S(1)}, u32[]{:S(2)}, u32[]{:S(2)}) collective-permute-start(f32[8,32,128]{2,1,0:T(8,128)S(1)} %fusion), channel_id=1, source_target_pairs={{0,8},{4,12},{8,0},{12,4},{16,24},{20,28},{24,16},{28,20},{1,9},{5... | collective-permute-start | bytes 393224 | tf_op jit(solution)/shard_map/ppermute | solution.py:156
  39.2 0.1 slice.7
  39.3 0.1 broadcast_in_dim.155
  39.4 0.2 select_reduce_fusion
  39.6 3.0 %collective-permute-done.7 = f32[8,32,128]{2,1,0:T(8,128)S(1)} collective-permute-done((f32[8,32,128]{2,1,0:T(8,128)S(1)}, f32[8,32,128]{2,1,0:T(8,128)S(1)}, u32[]{:S(2)}, u32[]{:S(2)}) %collective-permute-start.7) | collective-permute-done | bytes 131104 | tf_op jit(solution)/shard_map/ppermute | solution.py:156
  42.5 0.1 broadcast_select_fusion
  42.6 3.1 %collective-permute-start.8 = (f32[8,32,128]{2,1,0:T(8,128)S(1)}, f32[8,32,128]{2,1,0:T(8,128)S(1)}, u32[]{:S(2)}, u32[]{:S(2)}) collective-permute-start(f32[8,32,128]{2,1,0:T(8,128)S(1)} %broadcast_select_fusion), channel_id=1, source_target_pairs={{0,16},{4,20},{8,24},{12,28},{16,0},{20,4},{24,8},{28,12},{1,17},{... | collective-permute-start | bytes 393224 | tf_op jit(solution)/shard_map/ppermute | solution.py:156
  45.7 0.5 %broadcast_select_fusion.1 = s32[8]{0:T(128)} fusion(pred[8]{0:T(512)(128)(4,1)S(1)} %get-tuple-element.24, s32[8]{0:T(128)S(1)} %select_reduce_fusion), kind=kLoop, calls=%fused_computation.44 | loop fusion | flops 8 | bytes 72 | tf_op jit(solution)/shard_map/jit(_where)/select_n | solution.py:213
  46.2 2.4 %collective-permute-done.8 = f32[8,32,128]{2,1,0:T(8,128)S(1)} collective-permute-done((f32[8,32,128]{2,1,0:T(8,128)S(1)}, f32[8,32,128]{2,1,0:T(8,128)S(1)}, u32[]{:S(2)}, u32[]{:S(2)}) %collective-permute-start.8) | collective-permute-done | bytes 131104 | tf_op jit(solution)/shard_map/ppermute | solution.py:156
  48.7 0.7 %select_select_fusion = f32[8,32,128]{2,1,0:T(8,128)} fusion(f32[8,32,128]{2,1,0:T(8,128)S(1)} %collective-permute-done.8, f32[8,32,128]{2,1,0:T(8,128)S(1)} %broadcast_select_fusion, pred[8]{0:T(512)(128)(4,1)S(1)} %get-tuple-element.25, pred[8]{0:T(512)(128)(4,1)S(1)} %get-tuple-element.24), kind=kLoop, calls=%fused_computation.7 | loop fusion | flops 65536 | bytes 393232 | tf_op jit(solution)/shard_map/jit(_where)/select_n | solution.py:211
  (18 shorter events, 0.2 us)
Async XLA Ops:
  12.8 14.0 %collective-permute-start.4 = (f32[8,32,128]{2,1,0:T(8,128)S(1)}, f32[8,32,128]{2,1,0:T(8,128)S(1)}, u32[]{:S(2)}, u32[]{:S(2)}) collective-permute-start(f32[8,32,128]{2,1,0:T(8,128)S(1)} %get-tuple-element.11), channel_id=1, source_target_pairs={{0,1},{1,0},{2,3},{3,2},{4,5},{5,4},{6,7},{7,6},{8,9},{9,8},{10,11... | collective-permute-start | bytes 393224 | tf_op jit(solution)/shard_map/ppermute | solution.py:156
  13.3 15.7 %collective-permute-start.3 = (f32[8,32,128]{2,1,0:T(8,128)S(1)}, f32[8,32,128]{2,1,0:T(8,128)S(1)}, u32[]{:S(2)}, u32[]{:S(2)}) collective-permute-start(f32[8,32,128]{2,1,0:T(8,128)S(1)} %get-tuple-element.9), channel_id=1, source_target_pairs={{0,1},{1,0},{2,3},{3,2},{4,5},{5,4},{6,7},{7,6},{8,9},{9,8},{10,11... | collective-permute-start | bytes 393224 | tf_op jit(solution)/shard_map/ppermute | solution.py:156
  13.4 4.5 %collective-permute-start = (s32[1,128]{1,0:T(1,128)S(1)}, s32[1,128]{1,0:T(1,128)S(1)}, u32[]{:S(2)}, u32[]{:S(2)}) collective-permute-start(s32[1,128]{1,0:T(1,128)S(1)} %get-tuple-element.7), channel_id=1, source_target_pairs={{0,4},{4,0},{8,12},{12,8},{16,20},{20,16},{24,28},{28,24},{1,5},{5... | collective-permute-start | bytes 1544 | tf_op jit(solution)/shard_map/ppermute | solution.py:156
  17.9 3.7 %collective-permute-start.1 = (s32[2,128]{1,0:T(2,128)S(1)}, s32[2,128]{1,0:T(2,128)S(1)}, u32[]{:S(2)}, u32[]{:S(2)}) collective-permute-start(s32[2,128]{1,0:T(2,128)S(1)} %pad_add_fusion.2), channel_id=1, source_target_pairs={{0,8},{4,12},{8,0},{12,4},{16,24},{20,28},{24,16},{28,20},{1,9},{5... | collective-permute-start | bytes 3080 | tf_op jit(solution)/shard_map/ppermute | solution.py:156
  21.6 4.7 %collective-permute-start.2 = (s32[4,128]{1,0:T(4,128)S(1)}, s32[4,128]{1,0:T(4,128)S(1)}, u32[]{:S(2)}, u32[]{:S(2)}) collective-permute-start(s32[4,128]{1,0:T(4,128)S(1)} %pad_add_fusion.1), channel_id=1, source_target_pairs={{0,16},{4,20},{8,24},{12,28},{16,0},{20,4},{24,8},{28,12},{1,17},{... | collective-permute-start | bytes 6152 | tf_op jit(solution)/shard_map/ppermute | solution.py:156
  26.8 5.0 %collective-permute-start.5 = (f32[8,32,128]{2,1,0:T(8,128)S(1)}, f32[8,32,128]{2,1,0:T(8,128)S(1)}, u32[]{:S(2)}, u32[]{:S(2)}) collective-permute-start(f32[8,32,128]{2,1,0:T(8,128)S(1)} %add.165), channel_id=1, source_target_pairs={{0,2},{1,3},{2,0},{3,1},{4,6},{5,7},{6,4},{7,5},{8,10},{9,11},{10,... | collective-permute-start | bytes 393224 | tf_op jit(solution)/shard_map/ppermute | solution.py:156
  31.9 5.0 %collective-permute-start.6 = (f32[8,32,128]{2,1,0:T(8,128)S(1)}, f32[8,32,128]{2,1,0:T(8,128)S(1)}, u32[]{:S(2)}, u32[]{:S(2)}) collective-permute-start(f32[8,32,128]{2,1,0:T(8,128)S(1)} %add_add_fusion), channel_id=1, source_target_pairs={{0,4},{4,0},{8,12},{12,8},{16,20},{20,16},{24,28},{28,24},{1,5},{5... | collective-permute-start | bytes 393224 | tf_op jit(solution)/shard_map/ppermute | solution.py:156
  37.3 5.3 %collective-permute-start.7 = (f32[8,32,128]{2,1,0:T(8,128)S(1)}, f32[8,32,128]{2,1,0:T(8,128)S(1)}, u32[]{:S(2)}, u32[]{:S(2)}) collective-permute-start(f32[8,32,128]{2,1,0:T(8,128)S(1)} %fusion), channel_id=1, source_target_pairs={{0,8},{4,12},{8,0},{12,4},{16,24},{20,28},{24,16},{28,20},{1,9},{5... | collective-permute-start | bytes 393224 | tf_op jit(solution)/shard_map/ppermute | solution.py:156
  42.6 6.0 %collective-permute-start.8 = (f32[8,32,128]{2,1,0:T(8,128)S(1)}, f32[8,32,128]{2,1,0:T(8,128)S(1)}, u32[]{:S(2)}, u32[]{:S(2)}) collective-permute-start(f32[8,32,128]{2,1,0:T(8,128)S(1)} %broadcast_select_fusion), channel_id=1, source_target_pairs={{0,16},{4,20},{8,24},{12,28},{16,0},{20,4},{24,8},{28,12},{1,17},{... | collective-permute-start | bytes 393224 | tf_op jit(solution)/shard_map/ppermute | solution.py:156

commit v3 on v2

--- a/solution.py
+++ b/solution.py
@@ -10,7 +10,7 @@
 
 F32, BF16 = jnp.float32, jnp.bfloat16
 NT = (((1,), (1,)), ((), ()))
-GROUP = 32
+GROUP = 48
 
 
 def split(a):
@@ -36,6 +36,10 @@
     def copy(k):
         at = pl.ds(k * piece, piece)
         return pltpu.make_async_copy(a_hbm.at[at], a_buf.at[at], sems.at[k])
+
+    def copy_group(i):
+        at = pl.ds(i * group, group)
+        return pltpu.make_async_copy(a_hbm.at[at], a_buf.at[at], sems.at[per - 1 + i])
 
     small = [
         pltpu.make_async_copy(src, dst, small_sems.at[k])
@@ -52,8 +56,10 @@
     copy(0).start()
     for c in small[1:]:
         c.start()
-    for k in range(1, min(2, chunks) * per):
+    for k in range(1, per):
         copy(k).start()
+    if chunks > 1:
+        copy_group(1).start()
     for o in outs:
         o[...] = jnp.zeros_like(o)
     iota = lax.broadcasted_iota(jnp.int32, (n, n), 0)
@@ -97,13 +103,11 @@
         rows_step(g, first[g : g + 1], g)
 
     def step(i, carry):
-        for k in range(per):
-            copy(i * per + k).wait()
+        copy_group(i).wait()
 
         @pl.when(i + 1 < chunks)
         def _():
-            for k in range(per):
-                copy((i + 1) * per + k).start()
+            copy_group(i + 1).start()
 
         row_vecs, col_vecs = vectors(row_ref, i), vectors(col_ref, i - 1)
         for g in range(group):
@@ -123,8 +127,8 @@
     width = pl.cdiv(slots + 1, 128) * 128
     count, n, _ = a_blocks.shape
     rows = n // parts
-    piece = 8
-    group = max(g for g in range(piece, GROUP + 1, piece) if count % g == 0)
+    group = max(g for g in range(8, GROUP + 1, 8) if count % g == 0)
+    piece = group // 2 if group % 16 == 0 else group
     hbm = pl.BlockSpec(memory_space=pltpu.HBM)
     vmem = pl.BlockSpec(memory_space=pltpu.VMEM)
     return pl.pallas_call(
@@ -140,7 +144,7 @@
             pltpu.VMEM(col_map.shape, jnp.int32),
             pltpu.VMEM((count, n, n), F32),
             pltpu.VMEM((group, n, 2 * n), BF16),
-            pltpu.SemaphoreType.DMA((count // piece,)),
+            pltpu.SemaphoreType.DMA((group // piece + count // group - 1,)),
             pltpu.SemaphoreType.DMA((4,)),
         ],
         compiler_params=pltpu.CompilerParams(vmem_limit_bytes=24 << 20),

time: 49.8 us -> 48.1 us (0.966)
  Pallas kernels: 11.5 us -> 9.82 us
    pallas_call x1, Pallas kernels: 11.5 us -> 9.82 us  [coarsen(): pl.pallas_call(functools.partial(coarsen_body, group=group, piece=piece,...]
where the time goes in v3:
time: 48.1 us; the launch traced here: 47.7 us
  starting transfers between devices  17.5 us (36%)
  waiting for transfers between devices  15.7 us (33%)
  Pallas kernels  9.82 us (20%)
  other arithmetic  2.73 us (6%)
  between operations  1.4 us (3%)
  local copies, waits for them, and re-layouts  0.49 us (1%)
    ppermute x9, starting transfers between devices, exchange(): return lax.ppermute(x, axis, [(i, i ^ bit) for i in range(size)])  17.5 us
    ppermute x9, waiting for transfers between devices, exchange(): return lax.ppermute(x, axis, [(i, i ^ bit) for i in range(size)])  15.7 us
    pallas_call x1, Pallas kernels, coarsen(): pl.pallas_call(functools.partial(coarsen_body, group=group, piece=piece,...  9.82 us
  transfers between devices with their start and end apart: 9, of which 7 were waited for; matrix products, arithmetic and copies ran while one was open for 4% of the time, Pallas kernels for 0%

profile of v3, /device:TPU:0, one launch (start us, length us, event | category | flops | bytes accessed | tf_op | source)
XLA Modules:
  0.0 47.7 jit_solution(5956100429786613448)
XLA Ops:
  1.3 9.8 %coarsen.1 = (s32[1,128]{1,0:T(1,128)S(1)}, f32[8,32,128]{2,1,0:T(8,128)S(1)}, f32[8,32,128]{2,1,0:T(8,128)S(1)}, f32[8,32,128]{2,1,0:T(8,128)S(1)}, f32[8,32,128]{2,1,0:T(8,128)S(1)}) custom-call(s32[1]{0:T(128)S(6)} %copy.8.count_ref, s32[8]{0:T(128)} %weight_hbm.1, s32[192]{0:T(256)} %target_hbm.1, f32[192,128,128]{2,1,0:T(8,128)} %a_hbm.1, ...), custom_call_target="tpu_custom_call" | custom-call | flops 3221225472 | bytes 12582912 | tf_op jit(solution)/shard_map/coarsen/pallas_call | solution.py:134
  11.1 0.5 %collective-permute-start.4 = (f32[8,32,128]{2,1,0:T(8,128)S(1)}, f32[8,32,128]{2,1,0:T(8,128)S(1)}, u32[]{:S(2)}, u32[]{:S(2)}) collective-permute-start(f32[8,32,128]{2,1,0:T(8,128)S(1)} %get-tuple-element.11), channel_id=1, source_target_pairs={{0,1},{1,0},{2,3},{3,2},{4,5},{5,4},{6,7},{7,6},{8,9},{9,8},{10,11... | collective-permute-start | bytes 393224 | tf_op jit(solution)/shard_map/ppermute | solution.py:160
  11.7 0.1 collective-permute-start.3
  11.7 3.0 %collective-permute-start = (s32[1,128]{1,0:T(1,128)S(1)}, s32[1,128]{1,0:T(1,128)S(1)}, u32[]{:S(2)}, u32[]{:S(2)}) collective-permute-start(s32[1,128]{1,0:T(1,128)S(1)} %get-tuple-element.7), channel_id=1, source_target_pairs={{0,4},{4,0},{8,12},{12,8},{16,20},{20,16},{24,28},{28,24},{1,5},{5... | collective-permute-start | bytes 1544 | tf_op jit(solution)/shard_map/ppermute | solution.py:160
  14.7 0.1 iota_add_fusion
  14.8 1.5 %collective-permute-done = s32[1,128]{1,0:T(1,128)S(1)} collective-permute-done((s32[1,128]{1,0:T(1,128)S(1)}, s32[1,128]{1,0:T(1,128)S(1)}, u32[]{:S(2)}, u32[]{:S(2)}) %collective-permute-start) | collective-permute-done | bytes 544 | tf_op jit(solution)/shard_map/ppermute | solution.py:160
  16.2 2.2 %collective-permute-start.1 = (s32[2,128]{1,0:T(2,128)S(1)}, s32[2,128]{1,0:T(2,128)S(1)}, u32[]{:S(2)}, u32[]{:S(2)}) collective-permute-start(s32[2,128]{1,0:T(2,128)S(1)} %pad_add_fusion.2), channel_id=1, source_target_pairs={{0,8},{4,12},{8,0},{12,4},{16,24},{20,28},{24,16},{28,20},{1,9},{5... | collective-permute-start | bytes 3080 | tf_op jit(solution)/shard_map/ppermute | solution.py:160
  18.4 1.5 %collective-permute-done.1 = s32[2,128]{1,0:T(2,128)S(1)} collective-permute-done((s32[2,128]{1,0:T(2,128)S(1)}, s32[2,128]{1,0:T(2,128)S(1)}, u32[]{:S(2)}, u32[]{:S(2)}) %collective-permute-start.1) | collective-permute-done | bytes 1056 | tf_op jit(solution)/shard_map/ppermute | solution.py:160
  20.0 3.1 %collective-permute-start.2 = (s32[4,128]{1,0:T(4,128)S(1)}, s32[4,128]{1,0:T(4,128)S(1)}, u32[]{:S(2)}, u32[]{:S(2)}) collective-permute-start(s32[4,128]{1,0:T(4,128)S(1)} %pad_add_fusion.1), channel_id=1, source_target_pairs={{0,16},{4,20},{8,24},{12,28},{16,0},{20,4},{24,8},{28,12},{1,17},{... | collective-permute-start | bytes 6152 | tf_op jit(solution)/shard_map/ppermute | solution.py:160
  23.1 0.1 add.161
  23.1 1.5 %collective-permute-done.2 = s32[4,128]{1,0:T(4,128)S(1)} collective-permute-done((s32[4,128]{1,0:T(4,128)S(1)}, s32[4,128]{1,0:T(4,128)S(1)}, u32[]{:S(2)}, u32[]{:S(2)}) %collective-permute-start.2) | collective-permute-done | bytes 2080 | tf_op jit(solution)/shard_map/ppermute | solution.py:160
  24.6 0.1 slice_reduce_fusion
  24.8 0.2 select_reduce_fusion.1
  25.0 0.1 add_select_fusion
  25.0 0.1 select_n.97
  25.1 0.0 collective-permute-done.4
  25.2 1.8 %collective-permute-start.5 = (f32[8,32,128]{2,1,0:T(8,128)S(1)}, f32[8,32,128]{2,1,0:T(8,128)S(1)}, u32[]{:S(2)}, u32[]{:S(2)}) collective-permute-start(f32[8,32,128]{2,1,0:T(8,128)S(1)} %add.165), channel_id=1, source_target_pairs={{0,2},{1,3},{2,0},{3,1},{4,6},{5,7},{6,4},{7,5},{8,10},{9,11},{10,... | collective-permute-start | bytes 393224 | tf_op jit(solution)/shard_map/ppermute | solution.py:160
  27.0 0.3 and_reduce_fusion.3
  27.4 0.0 collective-permute-done.3
  27.4 2.8 %collective-permute-done.5 = f32[8,32,128]{2,1,0:T(8,128)S(1)} collective-permute-done((f32[8,32,128]{2,1,0:T(8,128)S(1)}, f32[8,32,128]{2,1,0:T(8,128)S(1)}, u32[]{:S(2)}, u32[]{:S(2)}) %collective-permute-start.5) | collective-permute-done | bytes 131104 | tf_op jit(solution)/shard_map/ppermute | solution.py:160
  30.2 1.8 %collective-permute-start.6 = (f32[8,32,128]{2,1,0:T(8,128)S(1)}, f32[8,32,128]{2,1,0:T(8,128)S(1)}, u32[]{:S(2)}, u32[]{:S(2)}) collective-permute-start(f32[8,32,128]{2,1,0:T(8,128)S(1)} %add_add_fusion), channel_id=1, source_target_pairs={{0,4},{4,0},{8,12},{12,8},{16,20},{20,16},{24,28},{28,24},{1,5},{5... | collective-permute-start | bytes 393224 | tf_op jit(solution)/shard_map/ppermute | solution.py:160
  32.1 0.1 bitcast_select_fusion.2
  32.2 0.1 bitcast_select_fusion.1
  32.3 3.0 %collective-permute-done.6 = f32[8,32,128]{2,1,0:T(8,128)S(1)} collective-permute-done((f32[8,32,128]{2,1,0:T(8,128)S(1)}, f32[8,32,128]{2,1,0:T(8,128)S(1)}, u32[]{:S(2)}, u32[]{:S(2)}) %collective-permute-start.6) | collective-permute-done | bytes 131104 | tf_op jit(solution)/shard_map/ppermute | solution.py:160
  35.3 0.1 bitcast_select_fusion.5
  35.4 0.1 bitcast_select_fusion.4
  35.5 0.1 fusion
  35.6 2.0 %collective-permute-start.7 = (f32[8,32,128]{2,1,0:T(8,128)S(1)}, f32[8,32,128]{2,1,0:T(8,128)S(1)}, u32[]{:S(2)}, u32[]{:S(2)}) collective-permute-start(f32[8,32,128]{2,1,0:T(8,128)S(1)} %fusion), channel_id=1, source_target_pairs={{0,8},{4,12},{8,0},{12,4},{16,24},{20,28},{24,16},{28,20},{1,9},{5... | collective-permute-start | bytes 393224 | tf_op jit(solution)/shard_map/ppermute | solution.py:160
  37.6 0.1 slice.7
  37.6 0.1 broadcast_in_dim.155
  37.7 0.2 select_reduce_fusion
  37.9 3.0 %collective-permute-done.7 = f32[8,32,128]{2,1,0:T(8,128)S(1)} collective-permute-done((f32[8,32,128]{2,1,0:T(8,128)S(1)}, f32[8,32,128]{2,1,0:T(8,128)S(1)}, u32[]{:S(2)}, u32[]{:S(2)}) %collective-permute-start.7) | collective-permute-done | bytes 131104 | tf_op jit(solution)/shard_map/ppermute | solution.py:160
  40.9 0.1 broadcast_select_fusion
  41.0 3.1 %collective-permute-start.8 = (f32[8,32,128]{2,1,0:T(8,128)S(1)}, f32[8,32,128]{2,1,0:T(8,128)S(1)}, u32[]{:S(2)}, u32[]{:S(2)}) collective-permute-start(f32[8,32,128]{2,1,0:T(8,128)S(1)} %broadcast_select_fusion), channel_id=1, source_target_pairs={{0,16},{4,20},{8,24},{12,28},{16,0},{20,4},{24,8},{28,12},{1,17},{... | collective-permute-start | bytes 393224 | tf_op jit(solution)/shard_map/ppermute | solution.py:160
  44.0 0.5 %broadcast_select_fusion.1 = s32[8]{0:T(128)} fusion(pred[8]{0:T(512)(128)(4,1)S(1)} %get-tuple-element.24, s32[8]{0:T(128)S(1)} %select_reduce_fusion), kind=kLoop, calls=%fused_computation.44 | loop fusion | flops 8 | bytes 72 | tf_op jit(solution)/shard_map/jit(_where)/select_n | solution.py:217
  44.6 2.4 %collective-permute-done.8 = f32[8,32,128]{2,1,0:T(8,128)S(1)} collective-permute-done((f32[8,32,128]{2,1,0:T(8,128)S(1)}, f32[8,32,128]{2,1,0:T(8,128)S(1)}, u32[]{:S(2)}, u32[]{:S(2)}) %collective-permute-start.8) | collective-permute-done | bytes 131104 | tf_op jit(solution)/shard_map/ppermute | solution.py:160
  47.0 0.7 %select_select_fusion = f32[8,32,128]{2,1,0:T(8,128)} fusion(f32[8,32,128]{2,1,0:T(8,128)S(1)} %collective-permute-done.8, f32[8,32,128]{2,1,0:T(8,128)S(1)} %broadcast_select_fusion, pred[8]{0:T(512)(128)(4,1)S(1)} %get-tuple-element.25, pred[8]{0:T(512)(128)(4,1)S(1)} %get-tuple-element.24), kind=kLoop, calls=%fused_computation.7 | loop fusion | flops 65536 | bytes 393232 | tf_op jit(solution)/shard_map/jit(_where)/select_n | solution.py:215
  (18 shorter events, 0.2 us)
Async XLA Ops:
  11.1 14.0 %collective-permute-start.4 = (f32[8,32,128]{2,1,0:T(8,128)S(1)}, f32[8,32,128]{2,1,0:T(8,128)S(1)}, u32[]{:S(2)}, u32[]{:S(2)}) collective-permute-start(f32[8,32,128]{2,1,0:T(8,128)S(1)} %get-tuple-element.11), channel_id=1, source_target_pairs={{0,1},{1,0},{2,3},{3,2},{4,5},{5,4},{6,7},{7,6},{8,9},{9,8},{10,11... | collective-permute-start | bytes 393224 | tf_op jit(solution)/shard_map/ppermute | solution.py:160
  11.7 15.7 %collective-permute-start.3 = (f32[8,32,128]{2,1,0:T(8,128)S(1)}, f32[8,32,128]{2,1,0:T(8,128)S(1)}, u32[]{:S(2)}, u32[]{:S(2)}) collective-permute-start(f32[8,32,128]{2,1,0:T(8,128)S(1)} %get-tuple-element.9), channel_id=1, source_target_pairs={{0,1},{1,0},{2,3},{3,2},{4,5},{5,4},{6,7},{7,6},{8,9},{9,8},{10,11... | collective-permute-start | bytes 393224 | tf_op jit(solution)/shard_map/ppermute | solution.py:160
  11.7 4.5 %collective-permute-start = (s32[1,128]{1,0:T(1,128)S(1)}, s32[1,128]{1,0:T(1,128)S(1)}, u32[]{:S(2)}, u32[]{:S(2)}) collective-permute-start(s32[1,128]{1,0:T(1,128)S(1)} %get-tuple-element.7), channel_id=1, source_target_pairs={{0,4},{4,0},{8,12},{12,8},{16,20},{20,16},{24,28},{28,24},{1,5},{5... | collective-permute-start | bytes 1544 | tf_op jit(solution)/shard_map/ppermute | solution.py:160
  16.2 3.7 %collective-permute-start.1 = (s32[2,128]{1,0:T(2,128)S(1)}, s32[2,128]{1,0:T(2,128)S(1)}, u32[]{:S(2)}, u32[]{:S(2)}) collective-permute-start(s32[2,128]{1,0:T(2,128)S(1)} %pad_add_fusion.2), channel_id=1, source_target_pairs={{0,8},{4,12},{8,0},{12,4},{16,24},{20,28},{24,16},{28,20},{1,9},{5... | collective-permute-start | bytes 3080 | tf_op jit(solution)/shard_map/ppermute | solution.py:160
  20.0 4.7 %collective-permute-start.2 = (s32[4,128]{1,0:T(4,128)S(1)}, s32[4,128]{1,0:T(4,128)S(1)}, u32[]{:S(2)}, u32[]{:S(2)}) collective-permute-start(s32[4,128]{1,0:T(4,128)S(1)} %pad_add_fusion.1), channel_id=1, source_target_pairs={{0,16},{4,20},{8,24},{12,28},{16,0},{20,4},{24,8},{28,12},{1,17},{... | collective-permute-start | bytes 6152 | tf_op jit(solution)/shard_map/ppermute | solution.py:160
  25.2 5.0 %collective-permute-start.5 = (f32[8,32,128]{2,1,0:T(8,128)S(1)}, f32[8,32,128]{2,1,0:T(8,128)S(1)}, u32[]{:S(2)}, u32[]{:S(2)}) collective-permute-start(f32[8,32,128]{2,1,0:T(8,128)S(1)} %add.165), channel_id=1, source_target_pairs={{0,2},{1,3},{2,0},{3,1},{4,6},{5,7},{6,4},{7,5},{8,10},{9,11},{10,... | collective-permute-start | bytes 393224 | tf_op jit(solution)/shard_map/ppermute | solution.py:160
  30.2 5.0 %collective-permute-start.6 = (f32[8,32,128]{2,1,0:T(8,128)S(1)}, f32[8,32,128]{2,1,0:T(8,128)S(1)}, u32[]{:S(2)}, u32[]{:S(2)}) collective-permute-start(f32[8,32,128]{2,1,0:T(8,128)S(1)} %add_add_fusion), channel_id=1, source_target_pairs={{0,4},{4,0},{8,12},{12,8},{16,20},{20,16},{24,28},{28,24},{1,5},{5... | collective-permute-start | bytes 393224 | tf_op jit(solution)/shard_map/ppermute | solution.py:160
  35.6 5.3 %collective-permute-start.7 = (f32[8,32,128]{2,1,0:T(8,128)S(1)}, f32[8,32,128]{2,1,0:T(8,128)S(1)}, u32[]{:S(2)}, u32[]{:S(2)}) collective-permute-start(f32[8,32,128]{2,1,0:T(8,128)S(1)} %fusion), channel_id=1, source_target_pairs={{0,8},{4,12},{8,0},{12,4},{16,24},{20,28},{24,16},{28,20},{1,9},{5... | collective-permute-start | bytes 393224 | tf_op jit(solution)/shard_map/ppermute | solution.py:160
  41.0 6.0 %collective-permute-start.8 = (f32[8,32,128]{2,1,0:T(8,128)S(1)}, f32[8,32,128]{2,1,0:T(8,128)S(1)}, u32[]{:S(2)}, u32[]{:S(2)}) collective-permute-start(f32[8,32,128]{2,1,0:T(8,128)S(1)} %broadcast_select_fusion), channel_id=1, source_target_pairs={{0,16},{4,20},{8,24},{12,28},{16,0},{20,4},{24,8},{28,12},{1,17},{... | collective-permute-start | bytes 393224 | tf_op jit(solution)/shard_map/ppermute | solution.py:160

commit v4 on v3

--- a/solution.py
+++ b/solution.py
@@ -171,7 +171,9 @@
 
     table, *outs = coarsen(counts, weights, target, a_blocks, row_map, col_map, parts, "narrow")
 
-    for bit in bits:
+    ranks = [0]
+    for bit in bits[:1] + bits[:0:-1]:
+        ranks += [i ^ bit for i in ranks]
         table = jnp.concatenate([table, exchange(table, "wide", bit)], 0)
 
     piece = list(outs)
@@ -182,7 +184,7 @@
     value = piece[0]
 
     count_of = table[:, 0]
-    owner = own ^ jnp.arange(nwide, dtype=jnp.int32)
+    owner = own ^ jnp.array(ranks, jnp.int32)
     later = owner[None, :] >= owner[:, None]
     start = nwide * slots - jnp.sum(jnp.where(later, count_of[None, :], 0), 1)
     slot = jnp.arange(slots, dtype=jnp.int32)

time: 48.1 us -> 47.7 us (level)
  no operation moved by 1% of the time
where the time goes in v4:
time: 47.7 us; the launch traced here: 47.3 us
  starting transfers between devices  17.6 us (37%)
  waiting for transfers between devices  15.3 us (32%)
  Pallas kernels  9.82 us (21%)
  other arithmetic  2.65 us (6%)
  between operations  1.43 us (3%)
  local copies, waits for them, and re-layouts  0.5 us (1%)
    ppermute x9, starting transfers between devices, exchange(): return lax.ppermute(x, axis, [(i, i ^ bit) for i in range(size)])  17.6 us
    ppermute x9, waiting for transfers between devices, exchange(): return lax.ppermute(x, axis, [(i, i ^ bit) for i in range(size)])  15.3 us
    pallas_call x1, Pallas kernels, coarsen(): pl.pallas_call(functools.partial(coarsen_body, group=group, piece=piece,...  9.82 us
  transfers between devices with their start and end apart: 9, of which 7 were waited for; matrix products, arithmetic and copies ran while one was open for 4% of the time, Pallas kernels for 0%

profile of v4, /device:TPU:0, one launch (start us, length us, event | category | flops | bytes accessed | tf_op | source)
XLA Modules:
  0.0 47.3 jit_solution(16083040724984361682)
XLA Ops:
  0.6 0.0 copy-start
  1.3 9.8 %coarsen.1 = (s32[1,128]{1,0:T(1,128)S(1)}, f32[8,32,128]{2,1,0:T(8,128)S(1)}, f32[8,32,128]{2,1,0:T(8,128)S(1)}, f32[8,32,128]{2,1,0:T(8,128)S(1)}, f32[8,32,128]{2,1,0:T(8,128)S(1)}) custom-call(s32[1]{0:T(128)S(6)} %copy.9.count_ref, s32[8]{0:T(128)} %weight_hbm.1, s32[192]{0:T(256)} %target_hbm.1, f32[192,128,128]{2,1,0:T(8,128)} %a_hbm.1, ...), custom_call_target="tpu_custom_call" | custom-call | flops 3221225472 | bytes 12582912 | tf_op jit(solution)/shard_map/coarsen/pallas_call | solution.py:134
  11.1 3.1 %collective-permute-start = (s32[1,128]{1,0:T(1,128)S(1)}, s32[1,128]{1,0:T(1,128)S(1)}, u32[]{:S(2)}, u32[]{:S(2)}) collective-permute-start(s32[1,128]{1,0:T(1,128)S(1)} %get-tuple-element.7), channel_id=1, source_target_pairs={{0,4},{4,0},{8,12},{12,8},{16,20},{20,16},{24,28},{28,24},{1,5},{5... | collective-permute-start | bytes 1544 | tf_op jit(solution)/shard_map/ppermute | solution.py:160
  14.2 0.0 collective-permute-start.4
  14.2 0.5 %collective-permute-start.3 = (f32[8,32,128]{2,1,0:T(8,128)S(1)}, f32[8,32,128]{2,1,0:T(8,128)S(1)}, u32[]{:S(2)}, u32[]{:S(2)}) collective-permute-start(f32[8,32,128]{2,1,0:T(8,128)S(1)} %get-tuple-element.9), channel_id=1, source_target_pairs={{0,1},{1,0},{2,3},{3,2},{4,5},{5,4},{6,7},{7,6},{8,9},{9,8},{10,11... | collective-permute-start | bytes 393224 | tf_op jit(solution)/shard_map/ppermute | solution.py:160
  14.7 1.0 %collective-permute-done = s32[1,128]{1,0:T(1,128)S(1)} collective-permute-done((s32[1,128]{1,0:T(1,128)S(1)}, s32[1,128]{1,0:T(1,128)S(1)}, u32[]{:S(2)}, u32[]{:S(2)}) %collective-permute-start) | collective-permute-done | bytes 544 | tf_op jit(solution)/shard_map/ppermute | solution.py:160
  15.8 3.2 %collective-permute-start.1 = (s32[2,128]{1,0:T(2,128)S(1)}, s32[2,128]{1,0:T(2,128)S(1)}, u32[]{:S(2)}, u32[]{:S(2)}) collective-permute-start(s32[2,128]{1,0:T(2,128)S(1)} %pad_add_fusion.2), channel_id=1, source_target_pairs={{0,16},{4,20},{8,24},{12,28},{16,0},{20,4},{24,8},{28,12},{1,17},{... | collective-permute-start | bytes 3080 | tf_op jit(solution)/shard_map/ppermute | solution.py:160
  18.9 0.0 copy-done
  18.9 1.5 %collective-permute-done.1 = s32[2,128]{1,0:T(2,128)S(1)} collective-permute-done((s32[2,128]{1,0:T(2,128)S(1)}, s32[2,128]{1,0:T(2,128)S(1)}, u32[]{:S(2)}, u32[]{:S(2)}) %collective-permute-start.1) | collective-permute-done | bytes 1056 | tf_op jit(solution)/shard_map/ppermute | solution.py:160
  20.5 2.0 %collective-permute-start.2 = (s32[4,128]{1,0:T(4,128)S(1)}, s32[4,128]{1,0:T(4,128)S(1)}, u32[]{:S(2)}, u32[]{:S(2)}) collective-permute-start(s32[4,128]{1,0:T(4,128)S(1)} %pad_add_fusion.1), channel_id=1, source_target_pairs={{0,8},{4,12},{8,0},{12,4},{16,24},{20,28},{24,16},{28,20},{1,9},{5... | collective-permute-start | bytes 6152 | tf_op jit(solution)/shard_map/ppermute | solution.py:160
  22.5 1.7 %collective-permute-done.2 = s32[4,128]{1,0:T(4,128)S(1)} collective-permute-done((s32[4,128]{1,0:T(4,128)S(1)}, s32[4,128]{1,0:T(4,128)S(1)}, u32[]{:S(2)}, u32[]{:S(2)}) %collective-permute-start.2) | collective-permute-done | bytes 2080 | tf_op jit(solution)/shard_map/ppermute | solution.py:160
  24.2 0.1 slice_reduce_fusion
  24.3 0.2 iota_add_fusion
  24.5 0.1 add_select_fusion
  24.5 0.1 select_n.97
  24.6 0.1 add.161
  24.7 0.0 collective-permute-done.4
  24.8 1.8 %collective-permute-start.5 = (f32[8,32,128]{2,1,0:T(8,128)S(1)}, f32[8,32,128]{2,1,0:T(8,128)S(1)}, u32[]{:S(2)}, u32[]{:S(2)}) collective-permute-start(f32[8,32,128]{2,1,0:T(8,128)S(1)} %add.165), channel_id=1, source_target_pairs={{0,2},{1,3},{2,0},{3,1},{4,6},{5,7},{6,4},{7,5},{8,10},{9,11},{10,... | collective-permute-start | bytes 393224 | tf_op jit(solution)/shard_map/ppermute | solution.py:160
  26.6 0.3 and_reduce_fusion.3
  26.9 0.0 collective-permute-done.3
  27.0 2.8 %collective-permute-done.5 = f32[8,32,128]{2,1,0:T(8,128)S(1)} collective-permute-done((f32[8,32,128]{2,1,0:T(8,128)S(1)}, f32[8,32,128]{2,1,0:T(8,128)S(1)}, u32[]{:S(2)}, u32[]{:S(2)}) %collective-permute-start.5) | collective-permute-done | bytes 131104 | tf_op jit(solution)/shard_map/ppermute | solution.py:160
  29.8 1.8 %collective-permute-start.6 = (f32[8,32,128]{2,1,0:T(8,128)S(1)}, f32[8,32,128]{2,1,0:T(8,128)S(1)}, u32[]{:S(2)}, u32[]{:S(2)}) collective-permute-start(f32[8,32,128]{2,1,0:T(8,128)S(1)} %add_add_fusion), channel_id=1, source_target_pairs={{0,4},{4,0},{8,12},{12,8},{16,20},{20,16},{24,28},{28,24},{1,5},{5... | collective-permute-start | bytes 393224 | tf_op jit(solution)/shard_map/ppermute | solution.py:160
  31.7 0.1 bitcast_select_fusion.2
  31.8 0.1 bitcast_select_fusion.1
  31.9 3.0 %collective-permute-done.6 = f32[8,32,128]{2,1,0:T(8,128)S(1)} collective-permute-done((f32[8,32,128]{2,1,0:T(8,128)S(1)}, f32[8,32,128]{2,1,0:T(8,128)S(1)}, u32[]{:S(2)}, u32[]{:S(2)}) %collective-permute-start.6) | collective-permute-done | bytes 131104 | tf_op jit(solution)/shard_map/ppermute | solution.py:160
  34.9 0.1 bitcast_select_fusion.5
  35.0 0.1 bitcast_select_fusion.4
  35.1 0.1 fusion
  35.2 2.0 %collective-permute-start.7 = (f32[8,32,128]{2,1,0:T(8,128)S(1)}, f32[8,32,128]{2,1,0:T(8,128)S(1)}, u32[]{:S(2)}, u32[]{:S(2)}) collective-permute-start(f32[8,32,128]{2,1,0:T(8,128)S(1)} %fusion), channel_id=1, source_target_pairs={{0,8},{4,12},{8,0},{12,4},{16,24},{20,28},{24,16},{28,20},{1,9},{5... | collective-permute-start | bytes 393224 | tf_op jit(solution)/shard_map/ppermute | solution.py:160
  37.2 0.1 slice.7
  37.2 0.1 broadcast_in_dim.155
  37.3 0.2 select_reduce_fusion
  37.5 2.8 %collective-permute-done.7 = f32[8,32,128]{2,1,0:T(8,128)S(1)} collective-permute-done((f32[8,32,128]{2,1,0:T(8,128)S(1)}, f32[8,32,128]{2,1,0:T(8,128)S(1)}, u32[]{:S(2)}, u32[]{:S(2)}) %collective-permute-start.7) | collective-permute-done | bytes 131104 | tf_op jit(solution)/shard_map/ppermute | solution.py:160
  40.3 0.1 broadcast_select_fusion
  40.4 3.2 %collective-permute-start.8 = (f32[8,32,128]{2,1,0:T(8,128)S(1)}, f32[8,32,128]{2,1,0:T(8,128)S(1)}, u32[]{:S(2)}, u32[]{:S(2)}) collective-permute-start(f32[8,32,128]{2,1,0:T(8,128)S(1)} %broadcast_select_fusion), channel_id=1, source_target_pairs={{0,16},{4,20},{8,24},{12,28},{16,0},{20,4},{24,8},{28,12},{1,17},{... | collective-permute-start | bytes 393224 | tf_op jit(solution)/shard_map/ppermute | solution.py:160
  43.6 0.5 %broadcast_select_fusion.1 = s32[8]{0:T(128)} fusion(pred[8]{0:T(512)(128)(4,1)S(1)} %get-tuple-element.24, s32[8]{0:T(128)S(1)} %select_reduce_fusion), kind=kLoop, calls=%fused_computation.43 | loop fusion | flops 8 | bytes 72 | tf_op jit(solution)/shard_map/jit(_where)/select_n | solution.py:219
  44.2 2.4 %collective-permute-done.8 = f32[8,32,128]{2,1,0:T(8,128)S(1)} collective-permute-done((f32[8,32,128]{2,1,0:T(8,128)S(1)}, f32[8,32,128]{2,1,0:T(8,128)S(1)}, u32[]{:S(2)}, u32[]{:S(2)}) %collective-permute-start.8) | collective-permute-done | bytes 131104 | tf_op jit(solution)/shard_map/ppermute | solution.py:160
  46.6 0.7 %select_select_fusion = f32[8,32,128]{2,1,0:T(8,128)} fusion(f32[8,32,128]{2,1,0:T(8,128)S(1)} %collective-permute-done.8, f32[8,32,128]{2,1,0:T(8,128)S(1)} %broadcast_select_fusion, pred[8]{0:T(512)(128)(4,1)S(1)} %get-tuple-element.25, pred[8]{0:T(512)(128)(4,1)S(1)} %get-tuple-element.24), kind=kLoop, calls=%fused_computation.7 | loop fusion | flops 65536 | bytes 393232 | tf_op jit(solution)/shard_map/jit(_where)/select_n | solution.py:217
  (17 shorter events, 0.2 us)
Async XLA Ops:
  0.6 18.3 %copy-start = (s32[8]{0:T(128)S(1)}, s32[8]{0:T(128)}, u32[]{:S(2)}) copy-start(s32[8]{0:T(128)} %constant.20.clone) | copy-start | bytes 100
  11.1 4.6 %collective-permute-start = (s32[1,128]{1,0:T(1,128)S(1)}, s32[1,128]{1,0:T(1,128)S(1)}, u32[]{:S(2)}, u32[]{:S(2)}) collective-permute-start(s32[1,128]{1,0:T(1,128)S(1)} %get-tuple-element.7), channel_id=1, source_target_pairs={{0,4},{4,0},{8,12},{12,8},{16,20},{20,16},{24,28},{28,24},{1,5},{5... | collective-permute-start | bytes 1544 | tf_op jit(solution)/shard_map/ppermute | solution.py:160
  14.2 10.5 %collective-permute-start.4 = (f32[8,32,128]{2,1,0:T(8,128)S(1)}, f32[8,32,128]{2,1,0:T(8,128)S(1)}, u32[]{:S(2)}, u32[]{:S(2)}) collective-permute-start(f32[8,32,128]{2,1,0:T(8,128)S(1)} %get-tuple-element.11), channel_id=1, source_target_pairs={{0,1},{1,0},{2,3},{3,2},{4,5},{5,4},{6,7},{7,6},{8,9},{9,8},{10,11... | collective-permute-start | bytes 393224 | tf_op jit(solution)/shard_map/ppermute | solution.py:160
  14.2 12.7 %collective-permute-start.3 = (f32[8,32,128]{2,1,0:T(8,128)S(1)}, f32[8,32,128]{2,1,0:T(8,128)S(1)}, u32[]{:S(2)}, u32[]{:S(2)}) collective-permute-start(f32[8,32,128]{2,1,0:T(8,128)S(1)} %get-tuple-element.9), channel_id=1, source_target_pairs={{0,1},{1,0},{2,3},{3,2},{4,5},{5,4},{6,7},{7,6},{8,9},{9,8},{10,11... | collective-permute-start | bytes 393224 | tf_op jit(solution)/shard_map/ppermute | solution.py:160
  15.8 4.7 %collective-permute-start.1 = (s32[2,128]{1,0:T(2,128)S(1)}, s32[2,128]{1,0:T(2,128)S(1)}, u32[]{:S(2)}, u32[]{:S(2)}) collective-permute-start(s32[2,128]{1,0:T(2,128)S(1)} %pad_add_fusion.2), channel_id=1, source_target_pairs={{0,16},{4,20},{8,24},{12,28},{16,0},{20,4},{24,8},{28,12},{1,17},{... | collective-permute-start | bytes 3080 | tf_op jit(solution)/shard_map/ppermute | solution.py:160
  20.5 3.6 %collective-permute-start.2 = (s32[4,128]{1,0:T(4,128)S(1)}, s32[4,128]{1,0:T(4,128)S(1)}, u32[]{:S(2)}, u32[]{:S(2)}) collective-permute-start(s32[4,128]{1,0:T(4,128)S(1)} %pad_add_fusion.1), channel_id=1, source_target_pairs={{0,8},{4,12},{8,0},{12,4},{16,24},{20,28},{24,16},{28,20},{1,9},{5... | collective-permute-start | bytes 6152 | tf_op jit(solution)/shard_map/ppermute | solution.py:160
  24.8 5.0 %collective-permute-start.5 = (f32[8,32,128]{2,1,0:T(8,128)S(1)}, f32[8,32,128]{2,1,0:T(8,128)S(1)}, u32[]{:S(2)}, u32[]{:S(2)}) collective-permute-start(f32[8,32,128]{2,1,0:T(8,128)S(1)} %add.165), channel_id=1, source_target_pairs={{0,2},{1,3},{2,0},{3,1},{4,6},{5,7},{6,4},{7,5},{8,10},{9,11},{10,... | collective-permute-start | bytes 393224 | tf_op jit(solution)/shard_map/ppermute | solution.py:160
  29.8 5.0 %collective-permute-start.6 = (f32[8,32,128]{2,1,0:T(8,128)S(1)}, f32[8,32,128]{2,1,0:T(8,128)S(1)}, u32[]{:S(2)}, u32[]{:S(2)}) collective-permute-start(f32[8,32,128]{2,1,0:T(8,128)S(1)} %add_add_fusion), channel_id=1, source_target_pairs={{0,4},{4,0},{8,12},{12,8},{16,20},{20,16},{24,28},{28,24},{1,5},{5... | collective-permute-start | bytes 393224 | tf_op jit(solution)/shard_map/ppermute | solution.py:160
  35.2 5.1 %collective-permute-start.7 = (f32[8,32,128]{2,1,0:T(8,128)S(1)}, f32[8,32,128]{2,1,0:T(8,128)S(1)}, u32[]{:S(2)}, u32[]{:S(2)}) collective-permute-start(f32[8,32,128]{2,1,0:T(8,128)S(1)} %fusion), channel_id=1, source_target_pairs={{0,8},{4,12},{8,0},{12,4},{16,24},{20,28},{24,16},{28,20},{1,9},{5... | collective-permute-start | bytes 393224 | tf_op jit(solution)/shard_map/ppermute | solution.py:160
  40.4 6.2 %collective-permute-start.8 = (f32[8,32,128]{2,1,0:T(8,128)S(1)}, f32[8,32,128]{2,1,0:T(8,128)S(1)}, u32[]{:S(2)}, u32[]{:S(2)}) collective-permute-start(f32[8,32,128]{2,1,0:T(8,128)S(1)} %broadcast_select_fusion), channel_id=1, source_target_pairs={{0,16},{4,20},{8,24},{12,28},{16,0},{20,4},{24,8},{28,12},{1,17},{... | collective-permute-start | bytes 393224 | tf_op jit(solution)/shard_map/ppermute | solution.py:160
